TPU v7x, 256 devices: a whole 4x4x8 slice. The times are simulated.
256 devices in a mesh: tm: 64 (over z, y, core), site: 4 (over x).
Axes of the slice: x: 4, y: 4, z: 8, core: 2. Of those that a mesh axis runs over, the one named last changes fastest.
Arguments:
- obs_rows: bfloat16 [131072, 256], P(('tm', 'site')), may hold values from -2 to 2
- obs_values: bfloat16 [131072], P(('tm', 'site')), may hold values from -6 to 6
- obs_hours: int32 [131072], P(('tm', 'site')), may hold values from 0 to 3
- prior_precision: float32 [256, 256], replicated, may hold values from -1 to 3, as said below
- transition: float32 [256, 256], replicated, may hold values from -1 to 1
- site_basis: bfloat16 [1048576, 256], P(('tm', 'site')), may hold values from -0.375 to 0.375
Outputs:
- prediction: bfloat16 [256, 1048576], P(None, ('tm', 'site'))
Inputs may be any that keep to these rules, and one draw needn't show every extreme that they name: `prior_precision`: symmetric and positive definite.
All inputs are finite; a program needn't handle non-finite values. Where the computation divides by a largest or mean magnitude, that divisor is 1e-20 or more.
Results may differ from a plain program's by a relative error of at most 0.0049.
Values may be sent and summed in bfloat16 or wider, within the bound.
A program may use at most 64 MiB of HBM per device.

v0:
```python
import jax
import jax.numpy as jnp
from jax import lax
from jax.sharding import PartitionSpec as P

NS_ITERS = 8


def entering(part, axis, combine, identity):
    place = lax.axis_index(axis)
    gathered = jax.tree.map(lambda a: lax.all_gather(a, axis), part)
    state = jax.tree.map(lambda a, e: jnp.zeros_like(a) + jnp.asarray(e, a.dtype), part, identity)

    def one(turn, state):
        return combine(
            state, jax.tree.map(lambda a: lax.dynamic_index_in_dim(a, turn, 0, False), gathered)
        )

    return lax.fori_loop(0, place, one, state)


def approx_inverse(precisions):
    states = precisions.shape[-1]
    bounds = jnp.max(jnp.sum(jnp.abs(precisions), axis=2), axis=1)
    identity = jnp.eye(states, dtype=jnp.float32)
    inverse = identity[None] / bounds[:, None, None]
    for iteration in range(NS_ITERS):
        product = jnp.einsum("hij,hjk->hik", precisions, inverse, precision=lax.Precision.HIGHEST)
        inverse = jnp.einsum(
            "hij,hjk->hik", inverse, 2.0 * identity - product, precision=lax.Precision.HIGHEST
        )
    return inverse


def compose(earlier, latter):
    joined_map = jnp.dot(latter[0], earlier[0], precision=lax.Precision.HIGHEST)
    joined_shift = jnp.dot(latter[0], earlier[1], precision=lax.Precision.HIGHEST) + latter[1]
    return (joined_map, joined_shift)


def hour_elements(summed_grams, drives, prior_precision, coupled):
    inverse = approx_inverse(prior_precision[None] + summed_grams)
    hour_maps = jnp.einsum("hij,jk->hik", inverse, coupled, precision=lax.Precision.HIGHEST)
    offsets = jnp.einsum("hij,hj->hi", inverse, drives, precision=lax.Precision.HIGHEST)
    return (hour_maps, offsets)


def body(obs_rows, obs_values, obs_hours, prior_precision, transition, site_basis):
    blocks = lax.axis_size("site")
    row_count = obs_rows.shape[0]
    hour_slot = lax.broadcasted_iota(jnp.int32, (blocks, row_count), 0)
    member = obs_hours[None, :] == hour_slot
    masked = jnp.where(member[:, :, None], obs_rows[None], jnp.zeros((), jnp.bfloat16))
    local_grams = jnp.einsum("hrs,rt->hst", masked, obs_rows, preferred_element_type=jnp.float32)
    weighted = jnp.where(member, obs_values[None], jnp.zeros((), jnp.bfloat16))
    local_drives = jnp.einsum("hr,rs->hs", weighted, obs_rows, preferred_element_type=jnp.float32)
    summed_grams, drives = (
        lax.psum_scatter(local_grams, "site", scatter_dimension=0, tiled=True),
        lax.psum_scatter(local_drives, "site", scatter_dimension=0, tiled=True),
    )
    coupled = jnp.dot(prior_precision, transition, precision=lax.Precision.HIGHEST)
    states = transition.shape[0]
    identity = jnp.eye(states, dtype=jnp.float32)
    zero_state = jnp.zeros((states,), jnp.float32)
    hour_maps, offsets = hour_elements(summed_grams, drives, prior_precision, coupled)
    block_maps, block_offsets = (
        lax.all_gather(hour_maps, "site", axis=0, tiled=True),
        lax.all_gather(offsets, "site", axis=0, tiled=True),
    )
    joined = (block_maps[0], block_offsets[0])
    for position in range(1, blocks):
        joined = compose(joined, (block_maps[position], block_offsets[position]))
    before = entering(joined, "tm", compose, (identity, zero_state))
    state_mean = before[1]
    results = []
    for position in range(blocks):
        state_mean = (
            jnp.dot(block_maps[position], state_mean, precision=lax.Precision.HIGHEST)
            + block_offsets[position]
        )
        results.append(state_mean)
    rounded = jnp.stack(results).astype(jnp.bfloat16)
    return jnp.einsum(
        "hs,ns->hn",
        lax.all_gather(rounded, "tm", axis=0, tiled=True),
        site_basis,
        preferred_element_type=jnp.float32,
    ).astype(jnp.bfloat16)


def solution(mesh):
    in_specs = (
        P(("tm", "site"), None),
        P(("tm", "site")),
        P(("tm", "site")),
        P(),
        P(),
        P(("tm", "site"), None),
    )
    out_specs = P(None, ("tm", "site"))
    return jax.shard_map(body, mesh=mesh, in_specs=in_specs, out_specs=out_specs, check_vma=False)
```

profile of v0, /device:TPU:1, one launch (start us, length us, event | category | flops | bytes accessed | tf_op | source)
XLA Modules:
  0.0 322.2 jit_solution(5100696245763074373)
XLA Ops:
  6.5 1.2 copy.8
  7.8 0.7 iota_compare_fusion.3
  8.5 2.4 fusion.4
  11.3 28.3 %reduce-scatter.2.cloned.1.call-done = f32[1,256,256]{2,1,0:T(8,128)} async-done(((f32[4,256,256]{2,1,0:T(8,128)}), f32[1,256,256]{2,1,0:T(8,128)}) %reduce-scatter.2.cloned.1.call-update) | async-done | bytes 262160 | tf_op jit(solution)/shard_map/reduce_scatter | solution.py:58
  39.6 1.1 abs_reduce_fusion
  40.7 0.6 reduce_max.9
  42.7 0.4 convolution_subtract_fusion.6
  43.5 0.4 convolution_subtract_fusion.5
  48.2 1.1 fusion.69
  49.4 26.0 %all-gather.10.cloned.1.call-done = f32[1024,256]{1,0:T(8,128)} async-done(((f32[256,256]{1,0:T(8,128)}), f32[1024,256]{1,0:T(8,128)}) %all-gather.10.cloned.1.call-update) | async-done | bytes 1048592 | tf_op jit(solution)/shard_map/all_gather | solution.py:67
  75.3 1.5 fusion.21
  76.8 1.3 fusion.32
  78.2 2.0 fusion.38
  80.2 0.6 dynamic-slice
  80.8 1.1 fusion.46
  81.9 7.7 %all-reduce = f32[4,256]{1,0:T(4,128)S(1)} all-reduce(f32[4,256]{1,0:T(4,128)S(1)} %fusion.46), channel_id=7, replica_groups=mesh['tm'=64,'site'=4] {'site'}, use_global_device_ids=true, to_apply=%region_3.4.clone | all-reduce | flops 1024 | bytes 8192
  89.6 0.9 convolution_bitcast_fusion
  90.5 5.3 %all-gather.4 = f32[4,1,256]{2,1,0:T(1,128)S(1)} all-gather(f32[1,1,256]{2,1,0:T(1,128)S(1)} %convolution_bitcast_fusion), channel_id=4, replica_groups=mesh['tm'=64,'site'=4] {'site'}, dimensions={0}, use_global_device_ids=true | all-gather | bytes 5120 | tf_op jit(solution)/shard_map/all_gather | solution.py:68
  96.8 51.4 %all-gather.5 = f32[64,1,256]{2,1,0:T(1,128)S(1)} all-gather(f32[1,1,256]{2,1,0:T(1,128)S(1)} %bitcast.138), channel_id=5, replica_groups=mesh['tm'=64,'site'=4] {'tm'}, dimensions={0}, use_global_device_ids=true | all-gather | bytes 66560 | tf_op jit(solution)/shard_map/all_gather | solution.py:11
  148.1 34.4 %all-gather.12.cloned.1.call-done = f32[16384,256]{1,0:T(8,128)} async-done(((f32[256,256]{1,0:T(8,128)}), f32[16384,256]{1,0:T(8,128)}) %all-gather.12.cloned.1.call-update) | async-done | bytes 16777232 | tf_op jit(solution)/shard_map/all_gather | solution.py:11
  182.5 1.3 while.12
  182.5 1.2 fusion.114
  185.2 128.3 %all-gather.6 = bf16[64,4,256]{2,1,0:T(4,128)(2,1)S(1)} all-gather(bf16[1,4,256]{2,1,0:T(4,128)(2,1)S(1)} %maximum_bitcast_fusion), channel_id=1, replica_groups=mesh['tm'=64,'site'=4] {'tm'}, dimensions={0}, use_global_device_ids=true | all-gather | bytes 133120 | tf_op jit(solution)/shard_map/all_gather | solution.py:85
  313.6 2.1 convolution_convert_fusion
  (60 shorter events, 8.1 us)
Async XLA Ops:
  6.5 307.1 %copy-start = (bf16[4096,256]{1,0:T(8,128)(2,1)S(1)}, bf16[4096,256]{1,0:T(8,128)(2,1)}, u32[]{:S(2)}) copy-start(bf16[4096,256]{1,0:T(8,128)(2,1)} %param.13) | copy-start | bytes 6291460
  6.5 4.4 %copy-start.2 = (f32[256,256]{1,0:T(8,128)S(1)}, f32[256,256]{1,0:T(8,128)}, u32[]{:S(2)}) copy-start(f32[256,256]{1,0:T(8,128)} %param.11) | copy-start | bytes 786436
  6.5 4.4 %copy-start.3 = (f32[256,256]{1,0:T(8,128)S(1)}, f32[256,256]{1,0:T(8,128)}, u32[]{:S(2)}) copy-start(f32[256,256]{1,0:T(8,128)} %param.12) | copy-start | bytes 786436
  6.5 33.1 %reduce-scatter.2.cloned.1.call-start = ((), (), s32[]{:S(2)}) async-start(), calls=%async_computation.1 | async-start | bytes 1310720 | tf_op jit(solution)/shard_map/reduce_scatter | solution.py:58
  10.9 64.4 %all-gather.10.cloned.1.call-start = ((), (), s32[]{:S(2)}) async-start(), calls=%async_computation.2 | async-start | bytes 1310720 | tf_op jit(solution)/shard_map/all_gather | solution.py:67
  47.8 32.4 %copy-start.6 = (u32[256]{0:T(256)S(1)}, u32[256]{0:T(256)}, u32[]{:S(2)}) copy-start(u32[256]{0:T(256)} %constant.40) | copy-start | bytes 3076
  47.8 33.0 %copy-start.4 = (s32[512]{0:T(512)S(1)}, s32[512]{0:T(512)}, u32[]{:S(2)}) copy-start(s32[512]{0:T(512)} %param.10) | copy-start | bytes 6148
  47.8 33.0 %copy-start.5 = (bf16[512]{0:T(512)(128)(2,1)S(1)}, bf16[512]{0:T(512)(128)(2,1)}, u32[]{:S(2)}) copy-start(bf16[512]{0:T(512)(128)(2,1)} %param.9) | copy-start | bytes 3076
  49.3 133.2 %all-gather.12.cloned.1.call-start = ((), (), s32[]{:S(2)}) async-start(), calls=%async_computation.3 | async-start | bytes 17039360 | tf_op jit(solution)/shard_map/all_gather | solution.py:11
  75.3 20.5 %copy-start.1 = (f32[1024,256]{1,0:T(8,128)S(1)}, f32[1024,256]{1,0:T(8,128)}, u32[]{:S(2)}) copy-start(f32[1024,256]{1,0:T(8,128)} %all-gather.10.cloned.1.call-done) | copy-start | bytes 3145732
Sparse Core Ops, SparseCore 0:
  11.0 28.5 reduce-scatter.1
  49.4 25.8 all-gather.9
  80.3 102.1 all-gather.11
where the time goes:
time: 325 us; the launch traced here: 322 us
  blocking collectives  193 us (59%)
  waiting for transfers between devices  88.7 us (27%)
  matrix products  22.1 us (7%)
  between operations  14.3 us (4%)
    all_gather x1, blocking collectives, body(): lax.all_gather(rounded, 'tm', axis=0, tiled=True)  128 us
    all_gather x1, blocking collectives, entering(): gathered = jax.tree.map(lambda a: lax.all_gather(a, axis), part)  51.4 us
    all_gather x1, waiting for transfers between devices, entering(): gathered = jax.tree.map(lambda a: lax.all_gather(a, axis), part)  34.4 us
    reduce_scatter x1, waiting for transfers between devices, body(): lax.psum_scatter(local_grams, 'site', scatter_dimension=0, tiled=True)  28.3 us
    all_gather x1, waiting for transfers between devices, body(): lax.all_gather(hour_maps, 'site', axis=0, tiled=True)  26 us
    unnamed x1, blocking collectives  7.69 us
  transfers between devices with their start and end apart: 3, of which 3 were waited for; matrix products, arithmetic and copies ran while one was open for 1% of the time, Pallas kernels for 0%

commit v1 on v0

v1 whole, which is shorter than its diff:
```python
import jax
import jax.numpy as jnp
from jax import lax
from jax.experimental import pallas as pl
from jax.experimental.pallas import tpu as pltpu
from jax.sharding import PartitionSpec as P

F32, BF16 = jnp.float32, jnp.bfloat16
MESH = pl.DeviceIdType.MESH

S = 256
NS_ITERS = 8
HR = 4
PAD = 16
ROWS = S + PAD
NX, NY, NC, NZ = 4, 4, 2, 8
PLANE = NY * NC


def split(a):
    high = a.astype(BF16)
    return high, (a - high.astype(F32)).astype(BF16)


def mm(a, b):
    return jnp.dot(a, b, preferred_element_type=F32)


def dot3(a, b):
    ah, al = a
    bh, bl = b
    return mm(ah, bh) + mm(al, bh) + mm(ah, bl)


def wide(row):
    return jnp.broadcast_to(row, (PAD, S))


def kernel(
    rows_hbm, vals_hbm, hours_hbm, prior_hbm, trans_hbm,
    out_ref,
    xs, vs, hs, prior, trans, coupled, power, grams, drives, work, prefix, partner,
    ydiff, yoff, pre, full, handed, planemap, qhi, qlo, qoff, sin, sout, means,
    load_sem, xsend, xrecv, asend, arecv, csend, crecv, ysend, yrecv, osend, orecv,
    ssend, srecv, psend, precv, zsend, zrecv,
):
    tm = lax.axis_index("tm")
    x = lax.axis_index("site")
    spot = lax.rem(tm, PLANE)
    core = lax.rem(tm, NC)
    y = lax.div(spot, NC)
    z = lax.div(tm, PLANE)

    def at(zz, yy, cc):
        return zz * PLANE + yy * NC + cc

    loads = [
        pltpu.make_async_copy(rows_hbm.at[pl.ds(0, 256)], xs.at[3, 0], load_sem.at[0]),
        pltpu.make_async_copy(rows_hbm.at[pl.ds(256, 256)], xs.at[3, 1], load_sem.at[1]),
        pltpu.make_async_copy(vals_hbm, vs.at[3], load_sem.at[2]),
        pltpu.make_async_copy(hours_hbm, hs.at[3], load_sem.at[3]),
        pltpu.make_async_copy(prior_hbm, prior, load_sem.at[4]),
        pltpu.make_async_copy(trans_hbm, trans, load_sem.at[5]),
    ]
    for copy in loads:
        copy.start()

    barrier = pltpu.get_barrier_semaphore()
    greeted = [(tm, lax.rem(x + k, NX)) for k in range(1, NX)]
    greeted += [(z * PLANE + lax.rem(spot + k, PLANE), x) for k in range(1, PLANE)]
    greeted += [(lax.rem(z + k, NZ) * PLANE + spot, x) for k in range(1, NZ)]
    greeted += [(at(lax.rem(z + NZ + 1 - 2 * core, NZ), y, 1 - core), x)]
    for device in greeted:
        pl.semaphore_signal(barrier, inc=1, device_id=device, device_id_type=MESH)
    pl.semaphore_wait(barrier, len(greeted))

    started = []

    def remote(src, dst, send_sem, recv_sem, device):
        return pltpu.make_async_remote_copy(
            src_ref=src, dst_ref=dst, send_sem=send_sem, recv_sem=recv_sem,
            device_id=device, device_id_type=MESH,
        )

    def send(*args):
        copy = remote(*args)
        copy.start()
        started.append(copy)

    def arrived(ref, send_sem, recv_sem):
        remote(ref, ref, send_sem, recv_sem, (tm, x)).wait_recv()

    right, left, across = ((tm, lax.rem(x + k, NX)) for k in (1, 3, 2))
    for half in (0, 1):
        part = rows_hbm.at[pl.ds(half * 256, 256)]
        send(part, xs.at[0, half], xsend.at[0, half], xrecv.at[0, half], right)
        part = rows_hbm.at[pl.ds((1 - half) * 256, 256)]
        send(part, xs.at[1, 1 - half], xsend.at[1, 1 - half], xrecv.at[1, 1 - half], left)
    for slot, device in ((0, right), (1, left), (2, across)):
        send(vals_hbm, vs.at[slot], asend.at[0, slot], arecv.at[0, slot], device)
        send(hours_hbm, hs.at[slot], asend.at[1, slot], arecv.at[1, slot], device)

    for copy in loads:
        copy.wait()

    transposed = trans[...].T
    coupled[...] = dot3(split(transposed), split(prior[...]))
    power[...] = transposed
    for _ in range(3):
        parts = split(power[...])
        power[...] = dot3(parts, parts)

    def add_rows(slot, first):
        hour = hs[slot]
        value = vs[slot].astype(F32)
        sub = lax.broadcasted_iota(jnp.int32, (PAD, 512), 0)
        marked = jnp.where(sub == hour, value, 0.0).astype(BF16)
        shape = (2 * 256, S)
        block = xs[slot].reshape(shape)
        turned = block.T
        total = mm(marked, block)
        drives[...] = total if first else drives[...] + total
        for h in range(HR):
            member = jnp.where(hour == h, 1.0, 0.0).astype(BF16)
            product = mm(turned * member, block)
            grams[h] = product if first else grams[h] + product

    add_rows(3, True)
    arrived(xs.at[0, 0], xsend.at[0, 0], xrecv.at[0, 0])
    send(xs.at[0, 0], xs.at[2, 0], xsend.at[2, 0], xrecv.at[2, 0], right)
    arrived(xs.at[1, 1], xsend.at[1, 1], xrecv.at[1, 1])
    send(xs.at[1, 1], xs.at[2, 1], xsend.at[2, 1], xrecv.at[2, 1], left)
    for slot in range(3):
        arrived(vs.at[slot], asend.at[0, slot], arecv.at[0, slot])
        arrived(hs.at[slot], asend.at[1, slot], arecv.at[1, slot])
    arrived(xs.at[0, 1], xsend.at[0, 1], xrecv.at[0, 1])
    add_rows(0, False)
    arrived(xs.at[1, 0], xsend.at[1, 0], xrecv.at[1, 0])
    add_rows(1, False)
    arrived(xs.at[2, 0], xsend.at[2, 0], xrecv.at[2, 0])
    arrived(xs.at[2, 1], xsend.at[2, 1], xrecv.at[2, 1])
    add_rows(2, False)

    eye = (
        lax.broadcasted_iota(jnp.int32, (S, S), 0) == lax.broadcasted_iota(jnp.int32, (S, S), 1)
    ).astype(F32)
    for h in range(HR):
        lam = prior[...] + grams[h]
        bound = jnp.max(jnp.sum(jnp.abs(lam), axis=0, keepdims=True), axis=1, keepdims=True)
        scale = 1.0 / bound
        work[h, 0:S] = eye - lam * scale
        work[h, S:2 * S] = coupled[...] * scale
        work[h, 2 * S:2 * S + PAD] = drives[...] * scale

    def level(k, carry):
        for h in range(HR):
            held = work[h]
            parts = split(held)
            factor = (parts[0][0:S], parts[1][0:S])
            product = dot3(parts, factor)
            work[h, 0:S] = product[0:S]
            work[h, S:2 * S + PAD] = held[S:2 * S + PAD] + product[S:2 * S + PAD]
        return carry

    lax.fori_loop(0, NS_ITERS, level, 0)

    prefix[0, 0:S] = work[0, S:2 * S]
    prefix[0, S:ROWS] = wide(work[0, 2 * S:2 * S + 1])
    for h in range(1, HR):
        joined = dot3(split(prefix[h - 1]), split(work[h, S:2 * S]))
        prefix[h, 0:S] = joined[0:S]
        prefix[h, S:ROWS] = joined[S:ROWS] + wide(work[h, 2 * S + h:2 * S + h + 1])

    def after(earlier, later_map, later_off):
        joined = dot3(split(earlier), split(later_map))
        return joined[0:S], joined[S:ROWS] + wide(later_off)

    to_core0 = remote(prefix.at[HR - 1], partner, csend, crecv, (at(z, y, 0), x))
    to_core1 = remote(handed, full, psend.at[7], precv.at[7], (at(z, y, 1), x))

    def to_ring(src, dst, s, r, device):
        return remote(src, dst, s, r, device)

    y_right, y_left, y_across = ((at(z, lax.rem(y + k, NY), 0), x) for k in (1, 3, 2))
    ring = []
    for half in (0, 1):
        ring.append(to_ring(ydiff.at[y, half], ydiff.at[y, half], ysend.at[0, half], yrecv.at[0, half], y_right))
        ring.append(to_ring(ydiff.at[y, 1 - half], ydiff.at[y, 1 - half], ysend.at[1, 1 - half], yrecv.at[1, 1 - half], y_left))
    for slot, device in ((0, y_right), (1, y_left), (2, y_across)):
        ring.append(to_ring(yoff.at[y], yoff.at[y], osend.at[slot], orecv.at[slot], device))
    behind, ahead, opposite = (lax.rem(y + k, NY) for k in (3, 1, 2))
    ring_relay = [
        to_ring(ydiff.at[behind, 0], ydiff.at[behind, 0], ysend.at[2, 0], yrecv.at[2, 0], y_right),
        to_ring(ydiff.at[ahead, 1], ydiff.at[ahead, 1], ysend.at[2, 1], yrecv.at[2, 1], y_left),
    ]
    up = lax.rem(z + 1, NZ)
    steps = [
        remote(sout, sin, ssend.at[0], srecv, (at(up, y, 0), x)),
        remote(sout, sin, ssend.at[1], srecv, (at(up, y, 1), x)),
    ]

    def pass_on():
        for copy in steps:
            copy.start()

    def ready_means():
        for h in range(HR):
            m, o = after(full[...], prefix[h, 0:S], prefix[h, S:S + 1])
            high, low = split(m)
            qhi[h] = high
            qlo[h] = low
            qoff[h] = o[0:8]

    def apply(state, high, low):
        sh, sl = split(wide(state))
        both = mm(jnp.concatenate([sh, sl], axis=0), high)
        return both[0:1] + both[PAD:PAD + 1] + mm(sh, low)[0:1]

    @pl.when(core == 1)
    def _():
        to_core0.start()
        arrived(full, psend.at[7], precv.at[7])

    @pl.when(core == 0)
    def _():
        arrived(partner, csend, crecv)
        m, o = after(prefix[HR - 1], partner[0:S], partner[S:S + 1])
        diff = (power[...] - m).astype(BF16)
        ydiff[y, 0] = diff[0:128]
        ydiff[y, 1] = diff[128:256]
        yoff[y] = o[0:8]
        for copy in ring:
            copy.start()
        arrived(ydiff.at[behind, 0], ysend.at[0, 0], yrecv.at[0, 0])
        ring_relay[0].start()
        arrived(ydiff.at[ahead, 1], ysend.at[1, 1], yrecv.at[1, 1])
        ring_relay[1].start()
        arrived(ydiff.at[behind, 1], ysend.at[0, 1], yrecv.at[0, 1])
        arrived(ydiff.at[ahead, 0], ysend.at[1, 0], yrecv.at[1, 0])
        arrived(ydiff.at[opposite, 0], ysend.at[2, 0], yrecv.at[2, 0])
        arrived(ydiff.at[opposite, 1], ysend.at[2, 1], yrecv.at[2, 1])
        for slot, origin in ((0, behind), (1, ahead), (2, opposite)):
            arrived(yoff.at[origin], osend.at[slot], orecv.at[slot])

        def chip(j):
            return power[...] - ydiff[j].reshape(S, S).astype(F32), yoff[j, 0:1]

        pre[0, 0:S] = eye
        pre[0, S:ROWS] = jnp.zeros((PAD, S), F32)
        m, o = chip(0)
        pre[1, 0:S] = m
        pre[1, S:ROWS] = wide(o)
        for j in (1, 2, 3):
            m, o = after(pre[j], *chip(j))
            pre[j + 1, 0:S] = m
            pre[j + 1, S:ROWS] = o

        @pl.when(z == 0)
        def _():
            sout[...] = pre[NY, S:S + 1]
            pass_on()

        high, low = split(pre[NY, 0:S])
        planemap[0] = high
        planemap[1] = low
        full[...] = pre[y]
        m, o = after(pre[y], prefix[HR - 1, 0:S], prefix[HR - 1, S:S + 1])
        handed[0:S] = m
        handed[S:ROWS] = o
        to_core1.start()

    @pl.when(z >= 2)
    def _():
        ready_means()

    @pl.when(z == 0)
    def _():
        sin[...] = jnp.zeros((1, S), F32)

    @pl.when(z > 0)
    def _():
        arrived(sin, ssend.at[0], srecv)

    @pl.when(jnp.logical_and(core == 0, jnp.logical_and(z > 0, z < NZ - 1)))
    def _():
        sout[...] = apply(sin[...], planemap[0], planemap[1]) + pre[NY, S:S + 1]
        pass_on()

    @pl.when(z < 2)
    def _():
        ready_means()

    found = [apply(sin[...], qhi[h], qlo[h]) + qoff[h, 0:1] for h in range(HR)]
    means[tm] = jnp.concatenate(found, axis=0).astype(BF16)

    for k in range(1, PLANE):
        device = (z * PLANE + lax.rem(spot + k, PLANE), x)
        send(means.at[tm], means.at[tm], psend.at[k - 1], precv.at[k - 1], device)
    for k in range(1, PLANE):
        origin = z * PLANE + lax.rem(spot + PLANE - k, PLANE)
        arrived(means.at[origin], psend.at[k - 1], precv.at[k - 1])
    own = means.at[pl.ds(z * PLANE, PLANE)]
    for k in range(1, NZ):
        device = (lax.rem(z + k, NZ) * PLANE + spot, x)
        send(own, own, zsend.at[k - 1], zrecv.at[k - 1], device)
    for k in range(1, NZ):
        origin = lax.rem(z + NZ - k, NZ)
        arrived(means.at[pl.ds(origin * PLANE, PLANE)], zsend.at[k - 1], zrecv.at[k - 1])
    out_ref[...] = means[...]

    for copy in started:
        copy.wait_send()

    @pl.when(core == 1)
    def _():
        to_core0.wait_send()

    @pl.when(core == 0)
    def _():
        for copy in ring + ring_relay + [to_core1]:
            copy.wait_send()

    @pl.when(jnp.logical_and(core == 0, z < NZ - 1))
    def _():
        for copy in steps:
            copy.wait_send()


def filtered_means(obs_rows, obs_values, obs_hours, prior_precision, transition):
    any_space = pl.BlockSpec(memory_space=pl.ANY)
    dma = pltpu.SemaphoreType.DMA
    return pl.pallas_call(
        kernel,
        out_shape=jax.ShapeDtypeStruct((NZ * PLANE, HR, S), BF16),
        in_specs=[any_space] * 5,
        out_specs=pl.BlockSpec(memory_space=pltpu.VMEM),
        scratch_shapes=[
            pltpu.VMEM((4, 2, 256, S), BF16),
            pltpu.VMEM((4, 1, 512), BF16),
            pltpu.VMEM((4, 1, 512), jnp.int32),
            pltpu.VMEM((S, S), F32),
            pltpu.VMEM((S, S), F32),
            pltpu.VMEM((S, S), F32),
            pltpu.VMEM((S, S), F32),
            pltpu.VMEM((HR, S, S), F32),
            pltpu.VMEM((PAD, S), F32),
            pltpu.VMEM((HR, 2 * S + PAD, S), F32),
            pltpu.VMEM((HR, ROWS, S), F32),
            pltpu.VMEM((ROWS, S), F32),
            pltpu.VMEM((NY, 2, 128, S), BF16),
            pltpu.VMEM((NY, 8, S), F32),
            pltpu.VMEM((NY + 1, ROWS, S), F32),
            pltpu.VMEM((ROWS, S), F32),
            pltpu.VMEM((ROWS, S), F32),
            pltpu.VMEM((2, S, S), BF16),
            pltpu.VMEM((HR, S, S), BF16),
            pltpu.VMEM((HR, S, S), BF16),
            pltpu.VMEM((HR, 8, S), F32),
            pltpu.VMEM((1, S), F32),
            pltpu.VMEM((1, S), F32),
            pltpu.VMEM((NZ * PLANE, HR, S), BF16),
            dma((6,)),
            dma((3, 2)), dma((3, 2)),
            dma((2, 3)), dma((2, 3)),
            dma(()), dma(()),
            dma((3, 2)), dma((3, 2)),
            dma((3,)), dma((3,)),
            dma((2,)), dma(()),
            dma((8,)), dma((8,)),
            dma((7,)), dma((7,)),
        ],
        compiler_params=pltpu.CompilerParams(
            collective_id=0, has_side_effects=True, vmem_limit_bytes=32 * 1024 * 1024
        ),
    )(obs_rows, obs_values[None], obs_hours[None], prior_precision, transition)


def body(obs_rows, obs_values, obs_hours, prior_precision, transition, site_basis):
    means = filtered_means(obs_rows, obs_values, obs_hours, prior_precision, transition)
    return jnp.einsum(
        "hs,ns->hn", means.reshape(NZ * PLANE * HR, S), site_basis, preferred_element_type=F32
    ).astype(BF16)


def solution(mesh):
    in_specs = (
        P(("tm", "site"), None),
        P(("tm", "site")),
        P(("tm", "site")),
        P(),
        P(),
        P(("tm", "site"), None),
    )
    out_specs = P(None, ("tm", "site"))
    return jax.shard_map(body, mesh=mesh, in_specs=in_specs, out_specs=out_specs, check_vma=False)
```

time: 325 us -> 73.5 us (0.23)
  blocking collectives: 193 us -> 0 us
  waiting for transfers between devices: 88.7 us -> 0 us
  Pallas kernels: 0 us -> 66.8 us
  matrix products: 22.1 us -> 2.07 us
  between operations: 14.3 us -> 0.02 us
    all_gather x3 -> x0, blocking collectives: 185 us -> none  [the longest x1 128 us: body(): lax.all_gather(rounded, 'tm', axis=0, tiled=True)]
    pallas_call x0 -> x1, Pallas kernels: none -> 66.8 us  [filtered_means(): pl.pallas_call(kernel, out_shape=jax.ShapeDtypeStruct((NZ * PLANE, HR, S)...]
    all_gather x2 -> x0, waiting for transfers between devices: 60.3 us -> none  [the longest x1 34.4 us: entering(): gathered = jax.tree.map(lambda a: lax.all_gather(a, axis), part)]
    reduce_scatter x1 -> x0, waiting for transfers between devices: 28.3 us -> none  [body(): lax.psum_scatter(local_grams, 'site', scatter_dimension=0, tiled=True)]
    dot_general x33 -> x1, matrix products: 22.1 us -> 2.07 us  [body(): jnp.einsum('hs,ns->hn', means.reshape(NZ * PLANE * HR, S), site_basis, pr...]
    unnamed x1 -> x0, blocking collectives: 7.69 us -> none
  transfers between devices with their start and end apart: 3 -> 0, of which waited for: 3 -> 0; matrix products, arithmetic and copies ran while one was open for 1% -> 0% of each run, Pallas kernels for 0% -> 0%
where the time goes in v1:
time: 73.5 us; the launch traced here: 73.3 us
  Pallas kernels  66.8 us (91%)
  local copies, waits for them, and re-layouts  4.4 us (6%)
  matrix products  2.07 us (3%)
    pallas_call x1, Pallas kernels, filtered_means(): pl.pallas_call(kernel, out_shape=jax.ShapeDtypeStruct((NZ * PLANE, HR, S)...  66.8 us
    unnamed x10, local copies, waits for them, and re-layouts  3.53 us
    dot_general x1, matrix products, body(): jnp.einsum('hs,ns->hn', means.reshape(NZ * PLANE * HR, S), site_basis, pr...  2.07 us

profile of v1, /device:TPU:1, one launch (start us, length us, event | category | flops | bytes accessed | tf_op | source)
XLA Modules:
  0.0 73.3 jit_solution(11629861029795365001)
XLA Ops:
  0.0 0.0 copy-start
  0.0 0.8 %broadcast_in_dim.6.vals_hbm = bf16[1,512]{1,0:T(2,128)(2,1)S(1)} reshape(bf16[512]{0:T(512)(128)(2,1)} %param.7) | data formatting | bytes 2048 | tf_op jit(solution)/shard_map/broadcast_in_dim | solution.py:375
  0.8 0.0 copy-start.1
  0.8 0.9 %copy-done.1 = bf16[512,256]{1,0:T(8,128)(2,1)S(1)} copy-done((bf16[512,256]{1,0:T(8,128)(2,1)S(1)}, bf16[512,256]{1,0:T(8,128)(2,1)}, u32[]{:S(2)}) %copy-start.1) | copy-done | bytes 262168
  1.8 0.0 copy-start.2
  1.8 0.9 %copy-done.2 = f32[256,256]{1,0:T(8,128)S(1)} copy-done((f32[256,256]{1,0:T(8,128)S(1)}, f32[256,256]{1,0:T(8,128)}, u32[]{:S(2)}) %copy-start.2) | copy-done | bytes 262168
  2.7 0.0 copy-start.3
  2.7 0.9 %copy-done.3 = f32[256,256]{1,0:T(8,128)S(1)} copy-done((f32[256,256]{1,0:T(8,128)S(1)}, f32[256,256]{1,0:T(8,128)}, u32[]{:S(2)}) %copy-start.3) | copy-done | bytes 262168
  3.7 0.0 copy-start.4
  3.7 0.7 copy-done.4
  4.4 66.8 %shard_map.64 = bf16[64,4,256]{2,1,0:T(4,128)(2,1)S(1)} custom-call(bf16[512,256]{1,0:T(8,128)(2,1)S(1)} %copy-done.1, bf16[1,512]{1,0:T(2,128)(2,1)S(1)} %broadcast_in_dim.6.vals_hbm, s32[1,512]{1,0:T(1,128)S(1)} %bitcast.3, f32[256,256]{1,0:T(8,128)S(1)} %copy-done.2, f32[256,256]{1,0:T(8,128)S(1)} %copy-done.3), custom_call_target="tpu_custom_call" | custom-call | tf_op jit(solution)/shard_map/pallas_call | solution.py:332
  71.2 0.0 copy-done
  71.2 2.1 %convolution_convert_fusion = bf16[256,4096]{1,0:T(8,128)(2,1)} fusion(bf16[256,256]{1,0:T(8,128)(2,1)S(1)} %reshape.3, bf16[4096,256]{1,0:T(8,128)(2,1)S(1)} %copy-done), kind=kOutput, calls=%fused_computation | convolution fusion | flops 537919488 | bytes 4325376 | tf_op jit(solution)/shard_map/hs,ns->hn/dot_general | solution.py:380
  (1 shorter events, 0.0 us)
Async XLA Ops:
  0.0 71.2 %copy-start = (bf16[4096,256]{1,0:T(8,128)(2,1)S(1)}, bf16[4096,256]{1,0:T(8,128)(2,1)}, u32[]{:S(2)}) copy-start(bf16[4096,256]{1,0:T(8,128)(2,1)} %param.11) | copy-start | bytes 6291460
  0.8 0.9 %copy-start.1 = (bf16[512,256]{1,0:T(8,128)(2,1)S(1)}, bf16[512,256]{1,0:T(8,128)(2,1)}, u32[]{:S(2)}) copy-start(bf16[512,256]{1,0:T(8,128)(2,1)} %rows_hbm.1) | copy-start | bytes 786436
  1.8 0.9 %copy-start.2 = (f32[256,256]{1,0:T(8,128)S(1)}, f32[256,256]{1,0:T(8,128)}, u32[]{:S(2)}) copy-start(f32[256,256]{1,0:T(8,128)} %prior_hbm.1) | copy-start | bytes 786436
  2.7 0.9 %copy-start.3 = (f32[256,256]{1,0:T(8,128)S(1)}, f32[256,256]{1,0:T(8,128)}, u32[]{:S(2)}) copy-start(f32[256,256]{1,0:T(8,128)} %trans_hbm.1) | copy-start | bytes 786436
  3.7 0.7 copy-start.4

commit v2 on v1

--- a/solution.py
+++ b/solution.py
@@ -42,7 +42,7 @@
     xs, vs, hs, prior, trans, coupled, power, grams, drives, work, prefix, partner,
     ydiff, yoff, pre, full, handed, planemap, qhi, qlo, qoff, sin, sout, means,
     load_sem, xsend, xrecv, asend, arecv, csend, crecv, ysend, yrecv, osend, orecv,
-    ssend, srecv, psend, precv, zsend, zrecv,
+    ssend, srecv, psend, precv, zsend, zrecv, heard,
 ):
     tm = lax.axis_index("tm")
     x = lax.axis_index("site")
@@ -66,13 +66,20 @@
         copy.start()
 
     barrier = pltpu.get_barrier_semaphore()
-    greeted = [(tm, lax.rem(x + k, NX)) for k in range(1, NX)]
-    greeted += [(z * PLANE + lax.rem(spot + k, PLANE), x) for k in range(1, PLANE)]
-    greeted += [(lax.rem(z + k, NZ) * PLANE + spot, x) for k in range(1, NZ)]
-    greeted += [(at(lax.rem(z + NZ + 1 - 2 * core, NZ), y, 1 - core), x)]
+    near = [(at(z, y, 1 - core), x)]
+    near += [(at(z, lax.rem(y + k, NY), core), x) for k in (1, NY - 1)]
+    near += [(at(lax.rem(z + k, NZ), y, core), x) for k in (1, NZ - 1)]
+    greeted = [(tm, lax.rem(x + k, NX)) for k in (1, NX - 1)] + near
     for device in greeted:
         pl.semaphore_signal(barrier, inc=1, device_id=device, device_id_type=MESH)
     pl.semaphore_wait(barrier, len(greeted))
+
+    def tell(turn):
+        for device in near:
+            pl.semaphore_signal(heard.at[turn], inc=1, device_id=device, device_id_type=MESH)
+
+    def hear(turn):
+        pl.semaphore_wait(heard.at[turn], len(near))
 
     started = []
 
@@ -90,15 +97,16 @@
     def arrived(ref, send_sem, recv_sem):
         remote(ref, ref, send_sem, recv_sem, (tm, x)).wait_recv()
 
-    right, left, across = ((tm, lax.rem(x + k, NX)) for k in (1, 3, 2))
+    right, left = ((tm, lax.rem(x + k, NX)) for k in (1, 3))
     for half in (0, 1):
         part = rows_hbm.at[pl.ds(half * 256, 256)]
         send(part, xs.at[0, half], xsend.at[0, half], xrecv.at[0, half], right)
         part = rows_hbm.at[pl.ds((1 - half) * 256, 256)]
         send(part, xs.at[1, 1 - half], xsend.at[1, 1 - half], xrecv.at[1, 1 - half], left)
-    for slot, device in ((0, right), (1, left), (2, across)):
+    for slot, device in ((0, right), (1, left)):
         send(vals_hbm, vs.at[slot], asend.at[0, slot], arecv.at[0, slot], device)
         send(hours_hbm, hs.at[slot], asend.at[1, slot], arecv.at[1, slot], device)
+    tell(0)
 
     for copy in loads:
         copy.wait()
@@ -113,6 +121,7 @@
     def add_rows(slot, first):
         hour = hs[slot]
         value = vs[slot].astype(F32)
+        value = jnp.concatenate([value[i:i + 1] for i in range(4)], axis=1)
         sub = lax.broadcasted_iota(jnp.int32, (PAD, 512), 0)
         marked = jnp.where(sub == hour, value, 0.0).astype(BF16)
         shape = (2 * 256, S)
@@ -125,18 +134,33 @@
             product = mm(turned * member, block)
             grams[h] = product if first else grams[h] + product
 
+    hear(0)
+    tell(1)
     add_rows(3, True)
+    hear(1)
+    tell(2)
     arrived(xs.at[0, 0], xsend.at[0, 0], xrecv.at[0, 0])
     send(xs.at[0, 0], xs.at[2, 0], xsend.at[2, 0], xrecv.at[2, 0], right)
     arrived(xs.at[1, 1], xsend.at[1, 1], xrecv.at[1, 1])
     send(xs.at[1, 1], xs.at[2, 1], xsend.at[2, 1], xrecv.at[2, 1], left)
-    for slot in range(3):
+    for slot in range(2):
         arrived(vs.at[slot], asend.at[0, slot], arecv.at[0, slot])
         arrived(hs.at[slot], asend.at[1, slot], arecv.at[1, slot])
+    send(vs.at[0], vs.at[2], asend.at[0, 2], arecv.at[0, 2], right)
+    send(hs.at[0], hs.at[2], asend.at[1, 2], arecv.at[1, 2], right)
+    hear(2)
+    tell(3)
     arrived(xs.at[0, 1], xsend.at[0, 1], xrecv.at[0, 1])
     add_rows(0, False)
+    hear(3)
+    tell(4)
     arrived(xs.at[1, 0], xsend.at[1, 0], xrecv.at[1, 0])
     add_rows(1, False)
+    hear(4)
+    tell(5)
+    hear(5)
+    arrived(vs.at[2], asend.at[0, 2], arecv.at[0, 2])
+    arrived(hs.at[2], asend.at[1, 2], arecv.at[1, 2])
     arrived(xs.at[2, 0], xsend.at[2, 0], xrecv.at[2, 0])
     arrived(xs.at[2, 1], xsend.at[2, 1], xrecv.at[2, 1])
     add_rows(2, False)
@@ -291,25 +315,37 @@
         ready_means()
 
     found = [apply(sin[...], qhi[h], qlo[h]) + qoff[h, 0:1] for h in range(HR)]
-    means[tm] = jnp.concatenate(found, axis=0).astype(BF16)
-
-    for k in range(1, PLANE):
-        device = (z * PLANE + lax.rem(spot + k, PLANE), x)
-        send(means.at[tm], means.at[tm], psend.at[k - 1], precv.at[k - 1], device)
-    for k in range(1, PLANE):
-        origin = z * PLANE + lax.rem(spot + PLANE - k, PLANE)
-        arrived(means.at[origin], psend.at[k - 1], precv.at[k - 1])
-    own = means.at[pl.ds(z * PLANE, PLANE)]
-    for k in range(1, NZ):
+    means[z, spot] = jnp.concatenate(found, axis=0).astype(BF16)
+
+    for k in (4, 3, 5, 2, 6, 1, 7):
         device = (lax.rem(z + k, NZ) * PLANE + spot, x)
-        send(own, own, zsend.at[k - 1], zrecv.at[k - 1], device)
-    for k in range(1, NZ):
+        send(means.at[z, spot], means.at[z, spot], zsend.at[k - 1], zrecv.at[k - 1], device)
+
+    def spread(origin):
+        for j in range(1, PLANE):
+            device = (z * PLANE + lax.rem(spot + j, PLANE), x)
+            remote(
+                means.at[origin, spot], means.at[origin, spot],
+                psend.at[j - 1], precv.at[j - 1], device,
+            ).start()
+
+    spread(z)
+    for k in (1, 7, 2, 6, 3, 5, 4):
         origin = lax.rem(z + NZ - k, NZ)
-        arrived(means.at[pl.ds(origin * PLANE, PLANE)], zsend.at[k - 1], zrecv.at[k - 1])
+        arrived(means.at[origin, spot], zsend.at[k - 1], zrecv.at[k - 1])
+        spread(origin)
+    for j in range(1, PLANE):
+        origin = lax.rem(spot + PLANE - j, PLANE)
+        arrived(means.at[:, origin], psend.at[j - 1], precv.at[j - 1])
     out_ref[...] = means[...]
 
     for copy in started:
         copy.wait_send()
+    for j in range(1, PLANE):
+        device = (z * PLANE + lax.rem(spot + j, PLANE), x)
+        remote(
+            means.at[:, spot], means.at[:, spot], psend.at[j - 1], precv.at[j - 1], device
+        ).wait_send()
 
     @pl.when(core == 1)
     def _():
@@ -327,16 +363,16 @@
 
 
 def filtered_means(obs_rows, obs_values, obs_hours, prior_precision, transition):
-    any_space = pl.BlockSpec(memory_space=pl.ANY)
+    any_space = pl.BlockSpec(memory_space=pltpu.MemorySpace.HBM)
     dma = pltpu.SemaphoreType.DMA
     return pl.pallas_call(
         kernel,
-        out_shape=jax.ShapeDtypeStruct((NZ * PLANE, HR, S), BF16),
+        out_shape=jax.ShapeDtypeStruct((NZ, PLANE, HR, S), BF16),
         in_specs=[any_space] * 5,
         out_specs=pl.BlockSpec(memory_space=pltpu.VMEM),
         scratch_shapes=[
             pltpu.VMEM((4, 2, 256, S), BF16),
-            pltpu.VMEM((4, 1, 512), BF16),
+            pltpu.VMEM((4, 4, 128), BF16),
             pltpu.VMEM((4, 1, 512), jnp.int32),
             pltpu.VMEM((S, S), F32),
             pltpu.VMEM((S, S), F32),
@@ -358,7 +394,7 @@
             pltpu.VMEM((HR, 8, S), F32),
             pltpu.VMEM((1, S), F32),
             pltpu.VMEM((1, S), F32),
-            pltpu.VMEM((NZ * PLANE, HR, S), BF16),
+            pltpu.VMEM((NZ, PLANE, HR, S), BF16),
             dma((6,)),
             dma((3, 2)), dma((3, 2)),
             dma((2, 3)), dma((2, 3)),
@@ -368,11 +404,15 @@
             dma((2,)), dma(()),
             dma((8,)), dma((8,)),
             dma((7,)), dma((7,)),
+            pltpu.SemaphoreType.REGULAR((6,)),
         ],
         compiler_params=pltpu.CompilerParams(
             collective_id=0, has_side_effects=True, vmem_limit_bytes=32 * 1024 * 1024
         ),
-    )(obs_rows, obs_values[None], obs_hours[None], prior_precision, transition)
+    )(*(
+        pltpu.with_memory_space_constraint(a, pltpu.MemorySpace.HBM)
+        for a in (obs_rows, obs_values.reshape(4, 128), obs_hours[None], prior_precision, transition)
+    ))
 
 
 def body(obs_rows, obs_values, obs_hours, prior_precision, transition, site_basis):

time: 73.5 us -> 71.8 us (0.977)
  local copies, waits for them, and re-layouts: 4.4 us -> 0.04 us
  Pallas kernels: 66.8 us -> 69.5 us
    unnamed x10 -> x2, local copies, waits for them, and re-layouts: 3.53 us -> 0.01 us
    pallas_call x1, Pallas kernels: 66.8 us -> 69.5 us  [filtered_means(): pl.pallas_call(kernel, out_shape=jax.ShapeDtypeStruct((NZ, PLANE, HR, S),...]
    broadcast_in_dim x1 -> x0, local copies, waits for them, and re-layouts: 0.83 us -> none  [filtered_means(): obs_values[None]]
where the time goes in v2:
time: 71.8 us; the launch traced here: 71.7 us
  Pallas kernels  69.5 us (97%)
  matrix products  2.06 us (3%)
    pallas_call x1, Pallas kernels, filtered_means(): pl.pallas_call(kernel, out_shape=jax.ShapeDtypeStruct((NZ, PLANE, HR, S),...  69.5 us
    dot_general x1, matrix products, body(): jnp.einsum('hs,ns->hn', means.reshape(NZ * PLANE * HR, S), site_basis, pr...  2.06 us

profile of v2, /device:TPU:1, one launch (start us, length us, event | category | flops | bytes accessed | tf_op | source)
XLA Modules:
  0.0 71.7 jit_solution(4879344523351085246)
XLA Ops:
  0.0 0.0 copy-start
  0.0 69.5 %shard_map.64 = bf16[8,8,4,256]{3,2,1,0:T(4,128)(2,1)S(1)} custom-call(bf16[512,256]{1,0:T(8,128)(2,1)} %rows_hbm.1, bf16[4,128]{1,0:T(4,128)(2,1)} %bitcast.5, s32[1,512]{1,0:T(1,128)} %bitcast.4, f32[256,256]{1,0:T(8,128)} %prior_hbm.1, f32[256,256]{1,0:T(8,128)} %trans_hbm.1), custom_call_target="tpu_custom_call" | custom-call | tf_op jit(solution)/shard_map/pallas_call | solution.py:368
  69.6 0.0 copy-done
  69.6 2.1 %convolution_convert_fusion = bf16[256,4096]{1,0:T(8,128)(2,1)} fusion(bf16[256,256]{1,0:T(8,128)(2,1)S(1)} %reshape.7, bf16[4096,256]{1,0:T(8,128)(2,1)S(1)} %copy-done), kind=kOutput, calls=%fused_computation | convolution fusion | flops 537919488 | bytes 4325376 | tf_op jit(solution)/shard_map/hs,ns->hn/dot_general | solution.py:420
  (1 shorter events, 0.0 us)
Async XLA Ops:
  0.0 69.6 %copy-start = (bf16[4096,256]{1,0:T(8,128)(2,1)S(1)}, bf16[4096,256]{1,0:T(8,128)(2,1)}, u32[]{:S(2)}) copy-start(bf16[4096,256]{1,0:T(8,128)(2,1)} %param.11) | copy-start | bytes 6291460

commit v3 on v2

--- a/solution.py
+++ b/solution.py
@@ -68,18 +68,29 @@
     barrier = pltpu.get_barrier_semaphore()
     near = [(at(z, y, 1 - core), x)]
     near += [(at(z, lax.rem(y + k, NY), core), x) for k in (1, NY - 1)]
-    near += [(at(lax.rem(z + k, NZ), y, core), x) for k in (1, NZ - 1)]
-    greeted = [(tm, lax.rem(x + k, NX)) for k in (1, NX - 1)] + near
-    for device in greeted:
-        pl.semaphore_signal(barrier, inc=1, device_id=device, device_id_type=MESH)
-    pl.semaphore_wait(barrier, len(greeted))
+    beside = [(tm, lax.rem(x + k, NX)) for k in (1, NX - 1)]
+    inner = jnp.where(z > 0, 1, 0) + jnp.where(z < NZ - 1, 1, 0)
+
+    def greet(sem, devices):
+        for device in devices:
+            pl.semaphore_signal(sem, inc=1, device_id=device, device_id_type=MESH)
+
+        @pl.when(z > 0)
+        def _():
+            pl.semaphore_signal(sem, inc=1, device_id=(tm - PLANE, x), device_id_type=MESH)
+
+        @pl.when(z < NZ - 1)
+        def _():
+            pl.semaphore_signal(sem, inc=1, device_id=(tm + PLANE, x), device_id_type=MESH)
+
+    greet(barrier, beside + near)
+    pl.semaphore_wait(barrier, len(beside + near) + inner)
 
     def tell(turn):
-        for device in near:
-            pl.semaphore_signal(heard.at[turn], inc=1, device_id=device, device_id_type=MESH)
+        greet(heard.at[turn], near)
 
     def hear(turn):
-        pl.semaphore_wait(heard.at[turn], len(near))
+        pl.semaphore_wait(heard.at[turn], len(near) + inner)
 
     started = []
 
@@ -134,11 +145,7 @@
             product = mm(turned * member, block)
             grams[h] = product if first else grams[h] + product
 
-    hear(0)
-    tell(1)
     add_rows(3, True)
-    hear(1)
-    tell(2)
     arrived(xs.at[0, 0], xsend.at[0, 0], xrecv.at[0, 0])
     send(xs.at[0, 0], xs.at[2, 0], xsend.at[2, 0], xrecv.at[2, 0], right)
     arrived(xs.at[1, 1], xsend.at[1, 1], xrecv.at[1, 1])
@@ -148,23 +155,18 @@
         arrived(hs.at[slot], asend.at[1, slot], arecv.at[1, slot])
     send(vs.at[0], vs.at[2], asend.at[0, 2], arecv.at[0, 2], right)
     send(hs.at[0], hs.at[2], asend.at[1, 2], arecv.at[1, 2], right)
-    hear(2)
-    tell(3)
     arrived(xs.at[0, 1], xsend.at[0, 1], xrecv.at[0, 1])
     add_rows(0, False)
-    hear(3)
-    tell(4)
     arrived(xs.at[1, 0], xsend.at[1, 0], xrecv.at[1, 0])
     add_rows(1, False)
-    hear(4)
-    tell(5)
-    hear(5)
     arrived(vs.at[2], asend.at[0, 2], arecv.at[0, 2])
     arrived(hs.at[2], asend.at[1, 2], arecv.at[1, 2])
     arrived(xs.at[2, 0], xsend.at[2, 0], xrecv.at[2, 0])
     arrived(xs.at[2, 1], xsend.at[2, 1], xrecv.at[2, 1])
     add_rows(2, False)
 
+    hear(0)
+    tell(1)
     eye = (
         lax.broadcasted_iota(jnp.int32, (S, S), 0) == lax.broadcasted_iota(jnp.int32, (S, S), 1)
     ).astype(F32)
@@ -188,6 +190,8 @@
 
     lax.fori_loop(0, NS_ITERS, level, 0)
 
+    hear(1)
+    tell(2)
     prefix[0, 0:S] = work[0, S:2 * S]
     prefix[0, S:ROWS] = wide(work[0, 2 * S:2 * S + 1])
     for h in range(1, HR):
@@ -293,6 +297,8 @@
         handed[S:ROWS] = o
         to_core1.start()
 
+    hear(2)
+    tell(3)
     @pl.when(z >= 2)
     def _():
         ready_means()
@@ -310,6 +316,9 @@
         sout[...] = apply(sin[...], planemap[0], planemap[1]) + pre[NY, S:S + 1]
         pass_on()
 
+    hear(3)
+    tell(4)
+
     @pl.when(z < 2)
     def _():
         ready_means()
@@ -317,6 +326,9 @@
     found = [apply(sin[...], qhi[h], qlo[h]) + qoff[h, 0:1] for h in range(HR)]
     means[z, spot] = jnp.concatenate(found, axis=0).astype(BF16)
 
+    hear(4)
+    tell(5)
+    hear(5)
     for k in (4, 3, 5, 2, 6, 1, 7):
         device = (lax.rem(z + k, NZ) * PLANE + spot, x)
         send(means.at[z, spot], means.at[z, spot], zsend.at[k - 1], zrecv.at[k - 1], device)

time: 71.8 us -> 68.8 us (0.958)
  Pallas kernels: 69.5 us -> 66.6 us
    pallas_call x1, Pallas kernels: 69.5 us -> 66.6 us  [filtered_means(): pl.pallas_call(kernel, out_shape=jax.ShapeDtypeStruct((NZ, PLANE, HR, S),...]
where the time goes in v3:
time: 68.8 us; the launch traced here: 68.7 us
  Pallas kernels  66.6 us (97%)
  matrix products  2.06 us (3%)
    pallas_call x1, Pallas kernels, filtered_means(): pl.pallas_call(kernel, out_shape=jax.ShapeDtypeStruct((NZ, PLANE, HR, S),...  66.6 us
    dot_general x1, matrix products, body(): jnp.einsum('hs,ns->hn', means.reshape(NZ * PLANE * HR, S), site_basis, pr...  2.06 us

profile of v3, /device:TPU:1, one launch (start us, length us, event | category | flops | bytes accessed | tf_op | source)
XLA Modules:
  0.0 68.7 jit_solution(5118554190703057035)
XLA Ops:
  0.0 0.0 copy-start
  0.0 66.6 %shard_map.64 = bf16[8,8,4,256]{3,2,1,0:T(4,128)(2,1)S(1)} custom-call(bf16[512,256]{1,0:T(8,128)(2,1)} %rows_hbm.1, bf16[4,128]{1,0:T(4,128)(2,1)} %bitcast.5, s32[1,512]{1,0:T(1,128)} %bitcast.4, f32[256,256]{1,0:T(8,128)} %prior_hbm.1, f32[256,256]{1,0:T(8,128)} %trans_hbm.1), custom_call_target="tpu_custom_call" | custom-call | tf_op jit(solution)/shard_map/pallas_call | solution.py:380
  66.6 0.0 copy-done
  66.6 2.1 %convolution_convert_fusion = bf16[256,4096]{1,0:T(8,128)(2,1)} fusion(bf16[256,256]{1,0:T(8,128)(2,1)S(1)} %reshape.7, bf16[4096,256]{1,0:T(8,128)(2,1)S(1)} %copy-done), kind=kOutput, calls=%fused_computation | convolution fusion | flops 537919488 | bytes 4325376 | tf_op jit(solution)/shard_map/hs,ns->hn/dot_general | solution.py:432
  (1 shorter events, 0.0 us)
Async XLA Ops:
  0.0 66.6 %copy-start = (bf16[4096,256]{1,0:T(8,128)(2,1)S(1)}, bf16[4096,256]{1,0:T(8,128)(2,1)}, u32[]{:S(2)}) copy-start(bf16[4096,256]{1,0:T(8,128)(2,1)} %param.11) | copy-start | bytes 6291460

commit v4 on v3

--- a/solution.py
+++ b/solution.py
@@ -40,9 +40,10 @@
     rows_hbm, vals_hbm, hours_hbm, prior_hbm, trans_hbm,
     out_ref,
     xs, vs, hs, prior, trans, coupled, power, grams, drives, work, prefix, partner,
-    ydiff, yoff, pre, full, handed, planemap, qhi, qlo, qoff, sin, sout, means,
+    ydiff, yoff, pre, full, handed, planemap, planeoff, lower, lowermap, entry,
+    qhi, qlo, qoff, sin, sout, means,
     load_sem, xsend, xrecv, asend, arecv, csend, crecv, ysend, yrecv, osend, orecv,
-    ssend, srecv, psend, precv, zsend, zrecv, heard,
+    ssend, srecv, psend, precv, zsend, zrecv, msend, mrecv, heard,
 ):
     tm = lax.axis_index("tm")
     x = lax.axis_index("site")
@@ -146,6 +147,8 @@
             grams[h] = product if first else grams[h] + product
 
     add_rows(3, True)
+    hear(0)
+    tell(1)
     arrived(xs.at[0, 0], xsend.at[0, 0], xrecv.at[0, 0])
     send(xs.at[0, 0], xs.at[2, 0], xsend.at[2, 0], xrecv.at[2, 0], right)
     arrived(xs.at[1, 1], xsend.at[1, 1], xrecv.at[1, 1])
@@ -165,8 +168,8 @@
     arrived(xs.at[2, 1], xsend.at[2, 1], xrecv.at[2, 1])
     add_rows(2, False)
 
-    hear(0)
-    tell(1)
+    hear(1)
+    tell(2)
     eye = (
         lax.broadcasted_iota(jnp.int32, (S, S), 0) == lax.broadcasted_iota(jnp.int32, (S, S), 1)
     ).astype(F32)
@@ -186,12 +189,17 @@
             product = dot3(parts, factor)
             work[h, 0:S] = product[0:S]
             work[h, S:2 * S + PAD] = held[S:2 * S + PAD] + product[S:2 * S + PAD]
+
+        @pl.when(lax.rem(k, 2) == 1)
+        def _():
+            turn = 2 + lax.div(k, 2)
+            hear(turn)
+            tell(turn + 1)
+
         return carry
 
     lax.fori_loop(0, NS_ITERS, level, 0)
 
-    hear(1)
-    tell(2)
     prefix[0, 0:S] = work[0, S:2 * S]
     prefix[0, S:ROWS] = wide(work[0, 2 * S:2 * S + 1])
     for h in range(1, HR):
@@ -221,15 +229,20 @@
         to_ring(ydiff.at[behind, 0], ydiff.at[behind, 0], ysend.at[2, 0], yrecv.at[2, 0], y_right),
         to_ring(ydiff.at[ahead, 1], ydiff.at[ahead, 1], ysend.at[2, 1], yrecv.at[2, 1], y_left),
     ]
-    up = lax.rem(z + 1, NZ)
-    steps = [
-        remote(sout, sin, ssend.at[0], srecv, (at(up, y, 0), x)),
-        remote(sout, sin, ssend.at[1], srecv, (at(up, y, 1), x)),
+    def state_to(slot, zz, cc):
+        return remote(sout, sin, ssend.at[slot], srecv, (at(jnp.minimum(zz, NZ - 1), y, cc), x))
+
+    steps = [state_to(0, z + 1, 0), state_to(1, z + 1, 1)]
+    far_steps = [state_to(2, z + 2, 0), state_to(3, z + 2, 1)]
+    to_odd = [
+        remote(pre.at[NY], lower, msend.at[c], mrecv, (at(jnp.minimum(z + 1, NZ - 1), y, c), x))
+        for c in range(NC)
     ]
-
-    def pass_on():
-        for copy in steps:
-            copy.start()
+    odd = lax.rem(z, 2) == 1
+    paired = jnp.logical_and(odd, z >= 3)
+    lends = jnp.logical_and(jnp.logical_not(odd), z >= 2)
+    sends_state = jnp.logical_or(z == 0, jnp.logical_and(odd, z < NZ - 1))
+    sends_far = jnp.logical_and(odd, z < NZ - 1)
 
     def ready_means():
         for h in range(HR):
@@ -247,7 +260,6 @@
     @pl.when(core == 1)
     def _():
         to_core0.start()
-        arrived(full, psend.at[7], precv.at[7])
 
     @pl.when(core == 0)
     def _():
@@ -259,10 +271,24 @@
         yoff[y] = o[0:8]
         for copy in ring:
             copy.start()
+
+    hear(6)
+    tell(7)
+
+    @pl.when(core == 1)
+    def _():
+        hear(7)
+        tell(8)
+        arrived(full, psend.at[7], precv.at[7])
+
+    @pl.when(core == 0)
+    def _():
         arrived(ydiff.at[behind, 0], ysend.at[0, 0], yrecv.at[0, 0])
         ring_relay[0].start()
         arrived(ydiff.at[ahead, 1], ysend.at[1, 1], yrecv.at[1, 1])
         ring_relay[1].start()
+        hear(7)
+        tell(8)
         arrived(ydiff.at[behind, 1], ysend.at[0, 1], yrecv.at[0, 1])
         arrived(ydiff.at[ahead, 0], ysend.at[1, 0], yrecv.at[1, 0])
         arrived(ydiff.at[opposite, 0], ysend.at[2, 0], yrecv.at[2, 0])
@@ -286,23 +312,47 @@
         @pl.when(z == 0)
         def _():
             sout[...] = pre[NY, S:S + 1]
-            pass_on()
-
-        high, low = split(pre[NY, 0:S])
-        planemap[0] = high
-        planemap[1] = low
+            for copy in steps:
+                copy.start()
+
+        @pl.when(lends)
+        def _():
+            for copy in to_odd:
+                copy.start()
+
+        @pl.when(z == 1)
+        def _():
+            high, low = split(pre[NY, 0:S])
+            planemap[0] = high
+            planemap[1] = low
+            planeoff[...] = pre[NY, S:S + 1]
+
         full[...] = pre[y]
         m, o = after(pre[y], prefix[HR - 1, 0:S], prefix[HR - 1, S:S + 1])
         handed[0:S] = m
         handed[S:ROWS] = o
         to_core1.start()
 
-    hear(2)
-    tell(3)
+    hear(8)
     @pl.when(z >= 2)
     def _():
         ready_means()
 
+    @pl.when(paired)
+    def _():
+        arrived(lower, msend.at[0], mrecv)
+        high, low = split(lower[0:S])
+        lowermap[0] = high
+        lowermap[1] = low
+
+    @pl.when(jnp.logical_and(paired, core == 0))
+    def _():
+        m, o = after(lower[...], pre[NY, 0:S], pre[NY, S:S + 1])
+        high, low = split(m)
+        planemap[0] = high
+        planemap[1] = low
+        planeoff[...] = o[0:1]
+
     @pl.when(z == 0)
     def _():
         sin[...] = jnp.zeros((1, S), F32)
@@ -311,53 +361,47 @@
     def _():
         arrived(sin, ssend.at[0], srecv)
 
-    @pl.when(jnp.logical_and(core == 0, jnp.logical_and(z > 0, z < NZ - 1)))
-    def _():
-        sout[...] = apply(sin[...], planemap[0], planemap[1]) + pre[NY, S:S + 1]
-        pass_on()
-
-    hear(3)
-    tell(4)
+    entry[...] = sin[...]
+
+    @pl.when(jnp.logical_and(core == 0, sends_far))
+    def _():
+        sout[...] = apply(sin[...], planemap[0], planemap[1]) + planeoff[...]
+        for copy in far_steps + steps:
+            copy.start()
+
+    @pl.when(paired)
+    def _():
+        entry[...] = apply(sin[...], lowermap[0], lowermap[1]) + lower[S:S + 1]
 
     @pl.when(z < 2)
     def _():
         ready_means()
 
-    found = [apply(sin[...], qhi[h], qlo[h]) + qoff[h, 0:1] for h in range(HR)]
+    found = [apply(entry[...], qhi[h], qlo[h]) + qoff[h, 0:1] for h in range(HR)]
     means[z, spot] = jnp.concatenate(found, axis=0).astype(BF16)
 
-    hear(4)
-    tell(5)
-    hear(5)
+    mine = means.at[z, spot]
     for k in (4, 3, 5, 2, 6, 1, 7):
-        device = (lax.rem(z + k, NZ) * PLANE + spot, x)
-        send(means.at[z, spot], means.at[z, spot], zsend.at[k - 1], zrecv.at[k - 1], device)
-
-    def spread(origin):
-        for j in range(1, PLANE):
-            device = (z * PLANE + lax.rem(spot + j, PLANE), x)
-            remote(
-                means.at[origin, spot], means.at[origin, spot],
-                psend.at[j - 1], precv.at[j - 1], device,
-            ).start()
-
-    spread(z)
+        zz = lax.rem(z + k, NZ)
+        for j in range(PLANE):
+            device = (zz * PLANE + lax.rem(spot + j, PLANE), x)
+            remote(mine, mine, zsend.at[k - 1], zrecv.at[k - 1], device).start()
+    for j in range(1, PLANE):
+        device = (z * PLANE + lax.rem(spot + j, PLANE), x)
+        send(mine, mine, psend.at[j - 1], precv.at[j - 1], device)
+    for j in range(1, PLANE):
+        origin = lax.rem(spot + PLANE - j, PLANE)
+        arrived(means.at[z, origin], psend.at[j - 1], precv.at[j - 1])
     for k in (1, 7, 2, 6, 3, 5, 4):
         origin = lax.rem(z + NZ - k, NZ)
-        arrived(means.at[origin, spot], zsend.at[k - 1], zrecv.at[k - 1])
-        spread(origin)
-    for j in range(1, PLANE):
-        origin = lax.rem(spot + PLANE - j, PLANE)
-        arrived(means.at[:, origin], psend.at[j - 1], precv.at[j - 1])
+        arrived(means.at[origin], zsend.at[k - 1], zrecv.at[k - 1])
     out_ref[...] = means[...]
 
     for copy in started:
         copy.wait_send()
-    for j in range(1, PLANE):
-        device = (z * PLANE + lax.rem(spot + j, PLANE), x)
-        remote(
-            means.at[:, spot], means.at[:, spot], psend.at[j - 1], precv.at[j - 1], device
-        ).wait_send()
+    for k in range(1, NZ):
+        device = (lax.rem(z + k, NZ) * PLANE + spot, x)
+        remote(means.at[z], means.at[z], zsend.at[k - 1], zrecv.at[k - 1], device).wait_send()
 
     @pl.when(core == 1)
     def _():
@@ -368,9 +412,19 @@
         for copy in ring + ring_relay + [to_core1]:
             copy.wait_send()
 
-    @pl.when(jnp.logical_and(core == 0, z < NZ - 1))
+    @pl.when(jnp.logical_and(core == 0, sends_state))
     def _():
         for copy in steps:
+            copy.wait_send()
+
+    @pl.when(jnp.logical_and(core == 0, sends_far))
+    def _():
+        for copy in far_steps:
+            copy.wait_send()
+
+    @pl.when(jnp.logical_and(core == 0, lends))
+    def _():
+        for copy in to_odd:
             copy.wait_send()
 
 
@@ -401,6 +455,10 @@
             pltpu.VMEM((ROWS, S), F32),
             pltpu.VMEM((ROWS, S), F32),
             pltpu.VMEM((2, S, S), BF16),
+            pltpu.VMEM((1, S), F32),
+            pltpu.VMEM((ROWS, S), F32),
+            pltpu.VMEM((2, S, S), BF16),
+            pltpu.VMEM((1, S), F32),
             pltpu.VMEM((HR, S, S), BF16),
             pltpu.VMEM((HR, S, S), BF16),
             pltpu.VMEM((HR, 8, S), F32),
@@ -413,10 +471,11 @@
             dma(()), dma(()),
             dma((3, 2)), dma((3, 2)),
             dma((3,)), dma((3,)),
-            dma((2,)), dma(()),
+            dma((4,)), dma(()),
             dma((8,)), dma((8,)),
             dma((7,)), dma((7,)),
-            pltpu.SemaphoreType.REGULAR((6,)),
+            dma((2,)), dma(()),
+            pltpu.SemaphoreType.REGULAR((9,)),
         ],
         compiler_params=pltpu.CompilerParams(
             collective_id=0, has_side_effects=True, vmem_limit_bytes=32 * 1024 * 1024

time: 68.8 us -> 63.1 us (0.917)
  Pallas kernels: 66.6 us -> 60.9 us
    pallas_call x1, Pallas kernels: 66.6 us -> 60.9 us  [filtered_means(): pl.pallas_call(kernel, out_shape=jax.ShapeDtypeStruct((NZ, PLANE, HR, S),...]
where the time goes in v4:
time: 63.1 us; the launch traced here: 63 us
  Pallas kernels  60.9 us (97%)
  matrix products  2.06 us (3%)
    pallas_call x1, Pallas kernels, filtered_means(): pl.pallas_call(kernel, out_shape=jax.ShapeDtypeStruct((NZ, PLANE, HR, S),...  60.9 us
    dot_general x1, matrix products, body(): jnp.einsum('hs,ns->hn', means.reshape(NZ * PLANE * HR, S), site_basis, pr...  2.06 us

profile of v4, /device:TPU:1, one launch (start us, length us, event | category | flops | bytes accessed | tf_op | source)
XLA Modules:
  0.0 63.0 jit_solution(7078304167988962444)
XLA Ops:
  0.0 0.0 copy-start
  0.0 60.9 %shard_map.64 = bf16[8,8,4,256]{3,2,1,0:T(4,128)(2,1)S(1)} custom-call(bf16[512,256]{1,0:T(8,128)(2,1)} %rows_hbm.1, bf16[4,128]{1,0:T(4,128)(2,1)} %bitcast.5, s32[1,512]{1,0:T(1,128)} %bitcast.4, f32[256,256]{1,0:T(8,128)} %prior_hbm.1, f32[256,256]{1,0:T(8,128)} %trans_hbm.1), custom_call_target="tpu_custom_call" | custom-call | tf_op jit(solution)/shard_map/pallas_call | solution.py:434
  60.9 0.0 copy-done
  60.9 2.1 %convolution_convert_fusion = bf16[256,4096]{1,0:T(8,128)(2,1)} fusion(bf16[256,256]{1,0:T(8,128)(2,1)S(1)} %reshape.7, bf16[4096,256]{1,0:T(8,128)(2,1)S(1)} %copy-done), kind=kOutput, calls=%fused_computation | convolution fusion | flops 537919488 | bytes 4325376 | tf_op jit(solution)/shard_map/hs,ns->hn/dot_general | solution.py:491
  (1 shorter events, 0.0 us)
Async XLA Ops:
  0.0 60.9 %copy-start = (bf16[4096,256]{1,0:T(8,128)(2,1)S(1)}, bf16[4096,256]{1,0:T(8,128)(2,1)}, u32[]{:S(2)}) copy-start(bf16[4096,256]{1,0:T(8,128)(2,1)} %param.11) | copy-start | bytes 6291460

commit v5 on v4

--- a/solution.py
+++ b/solution.py
@@ -198,37 +198,52 @@
 
         return carry
 
-    lax.fori_loop(0, NS_ITERS, level, 0)
-
-    prefix[0, 0:S] = work[0, S:2 * S]
-    prefix[0, S:ROWS] = wide(work[0, 2 * S:2 * S + 1])
-    for h in range(1, HR):
-        joined = dot3(split(prefix[h - 1]), split(work[h, S:2 * S]))
-        prefix[h, 0:S] = joined[0:S]
-        prefix[h, S:ROWS] = joined[S:ROWS] + wide(work[h, 2 * S + h:2 * S + h + 1])
+    lax.fori_loop(0, NS_ITERS - 2, level, 0)
+
+    def closing(h, last):
+        held = work[h]
+        high, low = split(held)
+        factor = high[0:S]
+        maps = jnp.concatenate([high[S:2 * S + PAD], low[S:2 * S + PAD]], axis=0)
+        both = mm(maps, factor)
+        if not last:
+            square = (factor, low[0:S])
+            work[h, 0:S] = dot3(square, square)
+        work[h, S:2 * S + PAD] = held[S:2 * S + PAD] + both[0:ROWS] + both[ROWS:2 * ROWS]
+
+    for h in range(HR):
+        closing(h, False)
+    hear(5)
+    tell(6)
+    for h in range(HR):
+        closing(h, True)
 
     def after(earlier, later_map, later_off):
         joined = dot3(split(earlier), split(later_map))
         return joined[0:S], joined[S:ROWS] + wide(later_off)
 
+    def hour(h):
+        return work[h, S:2 * S], work[h, 2 * S + h:2 * S + h + 1]
+
+    def put(ref, mapped):
+        ref[0:S] = mapped[0]
+        ref[S:ROWS] = mapped[1]
+
+    for h in (0, 2):
+        put(prefix.at[h], (hour(h)[0], wide(hour(h)[1])))
+    put(prefix.at[1], after(prefix[0], *hour(1)))
+    put(handed, after(prefix[2], *hour(3)))
+    put(prefix.at[3], after(prefix[1], handed[0:S], handed[S:S + 1]))
+
     to_core0 = remote(prefix.at[HR - 1], partner, csend, crecv, (at(z, y, 0), x))
     to_core1 = remote(handed, full, psend.at[7], precv.at[7], (at(z, y, 1), x))
 
-    def to_ring(src, dst, s, r, device):
-        return remote(src, dst, s, r, device)
-
     y_right, y_left, y_across = ((at(z, lax.rem(y + k, NY), 0), x) for k in (1, 3, 2))
     ring = []
-    for half in (0, 1):
-        ring.append(to_ring(ydiff.at[y, half], ydiff.at[y, half], ysend.at[0, half], yrecv.at[0, half], y_right))
-        ring.append(to_ring(ydiff.at[y, 1 - half], ydiff.at[y, 1 - half], ysend.at[1, 1 - half], yrecv.at[1, 1 - half], y_left))
-    for slot, device in ((0, y_right), (1, y_left), (2, y_across)):
-        ring.append(to_ring(yoff.at[y], yoff.at[y], osend.at[slot], orecv.at[slot], device))
+    for slot, device in ((2, y_across), (0, y_right), (1, y_left)):
+        ring.append(remote(yoff.at[y], yoff.at[y], osend.at[slot], orecv.at[slot], device))
+        ring.append(remote(ydiff.at[y], ydiff.at[y], ysend.at[slot], yrecv.at[slot], device))
     behind, ahead, opposite = (lax.rem(y + k, NY) for k in (3, 1, 2))
-    ring_relay = [
-        to_ring(ydiff.at[behind, 0], ydiff.at[behind, 0], ysend.at[2, 0], yrecv.at[2, 0], y_right),
-        to_ring(ydiff.at[ahead, 1], ydiff.at[ahead, 1], ysend.at[2, 1], yrecv.at[2, 1], y_left),
-    ]
     def state_to(slot, zz, cc):
         return remote(sout, sin, ssend.at[slot], srecv, (at(jnp.minimum(zz, NZ - 1), y, cc), x))
 
@@ -265,9 +280,7 @@
     def _():
         arrived(partner, csend, crecv)
         m, o = after(prefix[HR - 1], partner[0:S], partner[S:S + 1])
-        diff = (power[...] - m).astype(BF16)
-        ydiff[y, 0] = diff[0:128]
-        ydiff[y, 1] = diff[128:256]
+        ydiff[y] = (power[...] - m).astype(BF16)
         yoff[y] = o[0:8]
         for copy in ring:
             copy.start()
@@ -275,39 +288,31 @@
     hear(6)
     tell(7)
 
+    put(prefix.at[2], after(prefix[1], *hour(2)))
+    hear(7)
+    tell(8)
+
     @pl.when(core == 1)
     def _():
-        hear(7)
-        tell(8)
         arrived(full, psend.at[7], precv.at[7])
 
     @pl.when(core == 0)
     def _():
-        arrived(ydiff.at[behind, 0], ysend.at[0, 0], yrecv.at[0, 0])
-        ring_relay[0].start()
-        arrived(ydiff.at[ahead, 1], ysend.at[1, 1], yrecv.at[1, 1])
-        ring_relay[1].start()
-        hear(7)
-        tell(8)
-        arrived(ydiff.at[behind, 1], ysend.at[0, 1], yrecv.at[0, 1])
-        arrived(ydiff.at[ahead, 0], ysend.at[1, 0], yrecv.at[1, 0])
-        arrived(ydiff.at[opposite, 0], ysend.at[2, 0], yrecv.at[2, 0])
-        arrived(ydiff.at[opposite, 1], ysend.at[2, 1], yrecv.at[2, 1])
         for slot, origin in ((0, behind), (1, ahead), (2, opposite)):
             arrived(yoff.at[origin], osend.at[slot], orecv.at[slot])
+            arrived(ydiff.at[origin], ysend.at[slot], yrecv.at[slot])
 
         def chip(j):
-            return power[...] - ydiff[j].reshape(S, S).astype(F32), yoff[j, 0:1]
-
-        pre[0, 0:S] = eye
-        pre[0, S:ROWS] = jnp.zeros((PAD, S), F32)
+            return power[...] - ydiff[j].astype(F32), yoff[j, 0:1]
+
+        put(pre.at[0], (eye, jnp.zeros((PAD, S), F32)))
         m, o = chip(0)
-        pre[1, 0:S] = m
-        pre[1, S:ROWS] = wide(o)
-        for j in (1, 2, 3):
-            m, o = after(pre[j], *chip(j))
-            pre[j + 1, 0:S] = m
-            pre[j + 1, S:ROWS] = o
+        put(pre.at[1], (m, wide(o)))
+        put(pre.at[2], after(pre[1], *chip(1)))
+        m, o = chip(2)
+        put(pre.at[3], (m, wide(o)))
+        put(handed, after(pre[3], *chip(3)))
+        put(pre.at[4], after(pre[2], handed[0:S], handed[S:S + 1]))
 
         @pl.when(z == 0)
         def _():
@@ -327,10 +332,9 @@
             planemap[1] = low
             planeoff[...] = pre[NY, S:S + 1]
 
+        put(pre.at[3], after(pre[2], *chip(2)))
         full[...] = pre[y]
-        m, o = after(pre[y], prefix[HR - 1, 0:S], prefix[HR - 1, S:S + 1])
-        handed[0:S] = m
-        handed[S:ROWS] = o
+        put(handed, after(pre[y], prefix[HR - 1, 0:S], prefix[HR - 1, S:S + 1]))
         to_core1.start()
 
     hear(8)
@@ -409,7 +413,7 @@
 
     @pl.when(core == 0)
     def _():
-        for copy in ring + ring_relay + [to_core1]:
+        for copy in ring + [to_core1]:
             copy.wait_send()
 
     @pl.when(jnp.logical_and(core == 0, sends_state))
@@ -449,7 +453,7 @@
             pltpu.VMEM((HR, 2 * S + PAD, S), F32),
             pltpu.VMEM((HR, ROWS, S), F32),
             pltpu.VMEM((ROWS, S), F32),
-            pltpu.VMEM((NY, 2, 128, S), BF16),
+            pltpu.VMEM((NY, S, S), BF16),
             pltpu.VMEM((NY, 8, S), F32),
             pltpu.VMEM((NY + 1, ROWS, S), F32),
             pltpu.VMEM((ROWS, S), F32),
@@ -469,7 +473,7 @@
             dma((3, 2)), dma((3, 2)),
             dma((2, 3)), dma((2, 3)),
             dma(()), dma(()),
-            dma((3, 2)), dma((3, 2)),
+            dma((3,)), dma((3,)),
             dma((3,)), dma((3,)),
             dma((4,)), dma(()),
             dma((8,)), dma((8,)),

time: 63.1 us -> 62 us (0.983)
  Pallas kernels: 60.9 us -> 59.8 us
    pallas_call x1, Pallas kernels: 60.9 us -> 59.8 us  [filtered_means(): pl.pallas_call(kernel, out_shape=jax.ShapeDtypeStruct((NZ, PLANE, HR, S),...]
where the time goes in v5:
time: 62 us
  Pallas kernels  59.8 us (96%)
  matrix products  2.06 us (3%)
    pallas_call x1, Pallas kernels, filtered_means(): pl.pallas_call(kernel, out_shape=jax.ShapeDtypeStruct((NZ, PLANE, HR, S),...  59.8 us
    dot_general x1, matrix products, body(): jnp.einsum('hs,ns->hn', means.reshape(NZ * PLANE * HR, S), site_basis, pr...  2.06 us

profile of v5, /device:TPU:1, one launch (start us, length us, event | category | flops | bytes accessed | tf_op | source)
XLA Modules:
  0.0 62.0 jit_solution(4185881552833651402)
XLA Ops:
  0.0 0.0 copy-start
  0.0 59.8 %shard_map.64 = bf16[8,8,4,256]{3,2,1,0:T(4,128)(2,1)S(1)} custom-call(bf16[512,256]{1,0:T(8,128)(2,1)} %rows_hbm.1, bf16[4,128]{1,0:T(4,128)(2,1)} %bitcast.5, s32[1,512]{1,0:T(1,128)} %bitcast.4, f32[256,256]{1,0:T(8,128)} %prior_hbm.1, f32[256,256]{1,0:T(8,128)} %trans_hbm.1), custom_call_target="tpu_custom_call" | custom-call | tf_op jit(solution)/shard_map/pallas_call | solution.py:438
  59.9 0.0 copy-done
  59.9 2.1 %convolution_convert_fusion = bf16[256,4096]{1,0:T(8,128)(2,1)} fusion(bf16[256,256]{1,0:T(8,128)(2,1)S(1)} %reshape.7, bf16[4096,256]{1,0:T(8,128)(2,1)S(1)} %copy-done), kind=kOutput, calls=%fused_computation | convolution fusion | flops 537919488 | bytes 4325376 | tf_op jit(solution)/shard_map/hs,ns->hn/dot_general | solution.py:495
  (1 shorter events, 0.0 us)
Async XLA Ops:
  0.0 59.9 %copy-start = (bf16[4096,256]{1,0:T(8,128)(2,1)S(1)}, bf16[4096,256]{1,0:T(8,128)(2,1)}, u32[]{:S(2)}) copy-start(bf16[4096,256]{1,0:T(8,128)(2,1)} %param.11) | copy-start | bytes 6291460

commit v6 on v5

--- a/solution.py
+++ b/solution.py
@@ -67,31 +67,35 @@
         copy.start()
 
     barrier = pltpu.get_barrier_semaphore()
-    near = [(at(z, y, 1 - core), x)]
-    near += [(at(z, lax.rem(y + k, NY), core), x) for k in (1, NY - 1)]
     beside = [(tm, lax.rem(x + k, NX)) for k in (1, NX - 1)]
-    inner = jnp.where(z > 0, 1, 0) + jnp.where(z < NZ - 1, 1, 0)
-
-    def greet(sem, devices):
-        for device in devices:
-            pl.semaphore_signal(sem, inc=1, device_id=device, device_id_type=MESH)
-
-        @pl.when(z > 0)
+    beside += [(z * PLANE + lax.rem(spot + k, PLANE), x) for k in range(1, PLANE)]
+
+    def both_ways(sem, reach):
+        @pl.when(z >= reach)
         def _():
-            pl.semaphore_signal(sem, inc=1, device_id=(tm - PLANE, x), device_id_type=MESH)
-
-        @pl.when(z < NZ - 1)
+            pl.semaphore_signal(
+                sem, inc=1, device_id=(tm - reach * PLANE, x), device_id_type=MESH
+            )
+
+        @pl.when(z < NZ - reach)
         def _():
-            pl.semaphore_signal(sem, inc=1, device_id=(tm + PLANE, x), device_id_type=MESH)
-
-    greet(barrier, beside + near)
-    pl.semaphore_wait(barrier, len(beside + near) + inner)
+            pl.semaphore_signal(
+                sem, inc=1, device_id=(tm + reach * PLANE, x), device_id_type=MESH
+            )
+
+    def ways(reach):
+        return jnp.where(z >= reach, 1, 0) + jnp.where(z < NZ - reach, 1, 0)
+
+    for device in beside:
+        pl.semaphore_signal(barrier, inc=1, device_id=device, device_id_type=MESH)
+    both_ways(barrier, 1)
+    pl.semaphore_wait(barrier, len(beside) + ways(1))
 
     def tell(turn):
-        greet(heard.at[turn], near)
+        both_ways(heard.at[turn], 2 ** turn)
 
     def hear(turn):
-        pl.semaphore_wait(heard.at[turn], len(near) + inner)
+        pl.semaphore_wait(heard.at[turn], ways(2 ** turn))
 
     started = []
 
@@ -189,13 +193,6 @@
             product = dot3(parts, factor)
             work[h, 0:S] = product[0:S]
             work[h, S:2 * S + PAD] = held[S:2 * S + PAD] + product[S:2 * S + PAD]
-
-        @pl.when(lax.rem(k, 2) == 1)
-        def _():
-            turn = 2 + lax.div(k, 2)
-            hear(turn)
-            tell(turn + 1)
-
         return carry
 
     lax.fori_loop(0, NS_ITERS - 2, level, 0)
@@ -213,8 +210,6 @@
 
     for h in range(HR):
         closing(h, False)
-    hear(5)
-    tell(6)
     for h in range(HR):
         closing(h, True)
 
@@ -285,13 +280,8 @@
         for copy in ring:
             copy.start()
 
-    hear(6)
-    tell(7)
 
     put(prefix.at[2], after(prefix[1], *hour(2)))
-    hear(7)
-    tell(8)
-
     @pl.when(core == 1)
     def _():
         arrived(full, psend.at[7], precv.at[7])
@@ -337,7 +327,8 @@
         put(handed, after(pre[y], prefix[HR - 1, 0:S], prefix[HR - 1, S:S + 1]))
         to_core1.start()
 
-    hear(8)
+    hear(2)
+
     @pl.when(z >= 2)
     def _():
         ready_means()
@@ -479,7 +470,7 @@
             dma((8,)), dma((8,)),
             dma((7,)), dma((7,)),
             dma((2,)), dma(()),
-            pltpu.SemaphoreType.REGULAR((9,)),
+            pltpu.SemaphoreType.REGULAR((3,)),
         ],
         compiler_params=pltpu.CompilerParams(
             collective_id=0, has_side_effects=True, vmem_limit_bytes=32 * 1024 * 1024

time: 62 us -> 59.5 us (0.960)
  Pallas kernels: 59.8 us -> 57.3 us
    pallas_call x1, Pallas kernels: 59.8 us -> 57.3 us  [filtered_means(): pl.pallas_call(kernel, out_shape=jax.ShapeDtypeStruct((NZ, PLANE, HR, S),...]
where the time goes in v6:
time: 59.5 us; the launch traced here: 59.4 us
  Pallas kernels  57.3 us (96%)
  matrix products  2.06 us (3%)
    pallas_call x1, Pallas kernels, filtered_means(): pl.pallas_call(kernel, out_shape=jax.ShapeDtypeStruct((NZ, PLANE, HR, S),...  57.3 us
    dot_general x1, matrix products, body(): jnp.einsum('hs,ns->hn', means.reshape(NZ * PLANE * HR, S), site_basis, pr...  2.06 us

profile of v6, /device:TPU:1, one launch (start us, length us, event | category | flops | bytes accessed | tf_op | source)
XLA Modules:
  0.0 59.4 jit_solution(16582995899888479363)
XLA Ops:
  0.0 0.0 copy-start
  0.0 57.3 %shard_map.64 = bf16[8,8,4,256]{3,2,1,0:T(4,128)(2,1)S(1)} custom-call(bf16[512,256]{1,0:T(8,128)(2,1)} %rows_hbm.1, bf16[4,128]{1,0:T(4,128)(2,1)} %bitcast.5, s32[1,512]{1,0:T(1,128)} %bitcast.4, f32[256,256]{1,0:T(8,128)} %prior_hbm.1, f32[256,256]{1,0:T(8,128)} %trans_hbm.1), custom_call_target="tpu_custom_call" | custom-call | tf_op jit(solution)/shard_map/pallas_call | solution.py:429
  57.4 0.0 copy-done
  57.4 2.1 %convolution_convert_fusion = bf16[256,4096]{1,0:T(8,128)(2,1)} fusion(bf16[256,256]{1,0:T(8,128)(2,1)S(1)} %reshape.7, bf16[4096,256]{1,0:T(8,128)(2,1)S(1)} %copy-done), kind=kOutput, calls=%fused_computation | convolution fusion | flops 537919488 | bytes 4325376 | tf_op jit(solution)/shard_map/hs,ns->hn/dot_general | solution.py:486
  (1 shorter events, 0.0 us)
Async XLA Ops:
  0.0 57.4 %copy-start = (bf16[4096,256]{1,0:T(8,128)(2,1)S(1)}, bf16[4096,256]{1,0:T(8,128)(2,1)}, u32[]{:S(2)}) copy-start(bf16[4096,256]{1,0:T(8,128)(2,1)} %param.11) | copy-start | bytes 6291460

commit v7 on v6

--- a/solution.py
+++ b/solution.py
@@ -15,6 +15,7 @@
 ROWS = S + PAD
 NX, NY, NC, NZ = 4, 4, 2, 8
 PLANE = NY * NC
+CHUNKS, WIDTH = 8, 512
 
 
 def split(a):
@@ -37,8 +38,8 @@
 
 
 def kernel(
-    rows_hbm, vals_hbm, hours_hbm, prior_hbm, trans_hbm,
-    out_ref,
+    rows_hbm, vals_hbm, hours_hbm, prior_hbm, trans_hbm, sites_hbm,
+    out_ref, sites_out,
     xs, vs, hs, prior, trans, coupled, power, grams, drives, work, prefix, partner,
     ydiff, yoff, pre, full, handed, planemap, planeoff, lower, lowermap, entry,
     qhi, qlo, qoff, sin, sout, means,
@@ -63,6 +64,7 @@
         pltpu.make_async_copy(prior_hbm, prior, load_sem.at[4]),
         pltpu.make_async_copy(trans_hbm, trans, load_sem.at[5]),
     ]
+    held_sites = pltpu.make_async_copy(sites_hbm, sites_out, load_sem.at[6])
     for copy in loads:
         copy.start()
 
@@ -123,6 +125,7 @@
         send(vals_hbm, vs.at[slot], asend.at[0, slot], arecv.at[0, slot], device)
         send(hours_hbm, hs.at[slot], asend.at[1, slot], arecv.at[1, slot], device)
     tell(0)
+    held_sites.start()
 
     for copy in loads:
         copy.wait()
@@ -391,6 +394,7 @@
         origin = lax.rem(z + NZ - k, NZ)
         arrived(means.at[origin], zsend.at[k - 1], zrecv.at[k - 1])
     out_ref[...] = means[...]
+    held_sites.wait()
 
     for copy in started:
         copy.wait_send()
@@ -423,14 +427,17 @@
             copy.wait_send()
 
 
-def filtered_means(obs_rows, obs_values, obs_hours, prior_precision, transition):
+def filtered_means(obs_rows, obs_values, obs_hours, prior_precision, transition, site_basis):
     any_space = pl.BlockSpec(memory_space=pltpu.MemorySpace.HBM)
     dma = pltpu.SemaphoreType.DMA
     return pl.pallas_call(
         kernel,
-        out_shape=jax.ShapeDtypeStruct((NZ, PLANE, HR, S), BF16),
-        in_specs=[any_space] * 5,
-        out_specs=pl.BlockSpec(memory_space=pltpu.VMEM),
+        out_shape=(
+            jax.ShapeDtypeStruct((NZ, PLANE, HR, S), BF16),
+            jax.ShapeDtypeStruct(site_basis.shape, BF16),
+        ),
+        in_specs=[any_space] * 6,
+        out_specs=(pl.BlockSpec(memory_space=pltpu.VMEM),) * 2,
         scratch_shapes=[
             pltpu.VMEM((4, 2, 256, S), BF16),
             pltpu.VMEM((4, 4, 128), BF16),
@@ -460,7 +467,7 @@
             pltpu.VMEM((1, S), F32),
             pltpu.VMEM((1, S), F32),
             pltpu.VMEM((NZ, PLANE, HR, S), BF16),
-            dma((6,)),
+            dma((7,)),
             dma((3, 2)), dma((3, 2)),
             dma((2, 3)), dma((2, 3)),
             dma(()), dma(()),
@@ -477,15 +484,46 @@
         ),
     )(*(
         pltpu.with_memory_space_constraint(a, pltpu.MemorySpace.HBM)
-        for a in (obs_rows, obs_values.reshape(4, 128), obs_hours[None], prior_precision, transition)
+        for a in (obs_rows, obs_values.reshape(4, 128), obs_hours[None], prior_precision, transition, site_basis)
     ))
 
 
+def predict_kernel(means_ref, sites_ref, out_hbm, held, sems):
+    copies = []
+    for c in range(CHUNKS):
+        held[c] = lax.dot_general(
+            means_ref[...], sites_ref[c * WIDTH:(c + 1) * WIDTH, :],
+            (((1,), (1,)), ((), ())), preferred_element_type=F32,
+        ).astype(BF16)
+        copies.append(
+            pltpu.make_async_copy(held.at[c], out_hbm.at[:, pl.ds(c * WIDTH, WIDTH)], sems.at[c])
+        )
+        copies[-1].start()
+    for copy in copies:
+        copy.wait()
+
+
+def predict(means, site_basis):
+    vmem = pl.BlockSpec(memory_space=pltpu.MemorySpace.VMEM)
+    hours, sites = means.shape[0], site_basis.shape[0]
+    return pl.pallas_call(
+        predict_kernel,
+        out_shape=jax.ShapeDtypeStruct((hours, sites), BF16),
+        in_specs=[vmem, vmem],
+        out_specs=pl.BlockSpec(memory_space=pltpu.MemorySpace.HBM),
+        scratch_shapes=[
+            pltpu.VMEM((CHUNKS, hours, WIDTH), BF16),
+            pltpu.SemaphoreType.DMA((CHUNKS,)),
+        ],
+        compiler_params=pltpu.CompilerParams(vmem_limit_bytes=16 * 1024 * 1024),
+    )(means, site_basis)
+
+
 def body(obs_rows, obs_values, obs_hours, prior_precision, transition, site_basis):
-    means = filtered_means(obs_rows, obs_values, obs_hours, prior_precision, transition)
-    return jnp.einsum(
-        "hs,ns->hn", means.reshape(NZ * PLANE * HR, S), site_basis, preferred_element_type=F32
-    ).astype(BF16)
+    means, sites = filtered_means(
+        obs_rows, obs_values, obs_hours, prior_precision, transition, site_basis
+    )
+    return predict(means.reshape(NZ * PLANE * HR, S), sites)
 
 
 def solution(mesh):

time: 59.5 us -> 59 us (level)
  matrix products: 2.06 us -> 0 us
  Pallas kernels: 57.3 us -> 58.9 us
    dot_general x1 -> x0, matrix products: 2.06 us -> none  [body(): jnp.einsum('hs,ns->hn', means.reshape(NZ * PLANE * HR, S), site_basis, pr...]
    pallas_call x1 -> x2, Pallas kernels: 57.3 us -> 58.9 us  [the longest x1 57.3 us: filtered_means(): pl.pallas_call(kernel, out_shape=(jax.ShapeDtypeStruct((NZ, PLANE, HR, S)...]
where the time goes in v7:
time: 59 us
  Pallas kernels  58.9 us (100%)
    pallas_call x1, Pallas kernels, filtered_means(): pl.pallas_call(kernel, out_shape=(jax.ShapeDtypeStruct((NZ, PLANE, HR, S)...  57.3 us
    pallas_call x1, Pallas kernels, predict(): pl.pallas_call(predict_kernel, out_shape=jax.ShapeDtypeStruct((hours, sit...  1.64 us

profile of v7, /device:TPU:1, one launch (start us, length us, event | category | flops | bytes accessed | tf_op | source)
XLA Modules:
  0.0 59.0 jit_solution(13801171686949260661)
XLA Ops:
  0.0 57.3 %shard_map.64 = (bf16[8,8,4,256]{3,2,1,0:T(4,128)(2,1)S(1)}, bf16[4096,256]{1,0:T(8,128)(2,1)S(1)}) custom-call(bf16[512,256]{1,0:T(8,128)(2,1)} %rows_hbm.1, bf16[4,128]{1,0:T(4,128)(2,1)} %bitcast.3, s32[1,512]{1,0:T(1,128)} %bitcast.2, f32[256,256]{1,0:T(8,128)} %prior_hbm.1, f32[256,256]{1,0:T(8,128)} %trans_hbm.1, bf16[4096,256]{1,0:T(8,128)(2,1)} %sites_hbm.1), custom_call_target="tpu_custom_call" | custom-call | tf_op jit(solution)/shard_map/pallas_call | solution.py:433
  57.3 1.6 %shard_map.65 = bf16[256,4096]{1,0:T(8,128)(2,1)} custom-call(bf16[256,256]{1,0:T(8,128)(2,1)S(1)} %reshape.7.means_ref, bf16[4096,256]{1,0:T(8,128)(2,1)S(1)} %get-tuple-element.8.sites_ref), custom_call_target="tpu_custom_call" | custom-call | tf_op jit(solution)/shard_map/pallas_call | solution.py:509
  (1 shorter events, 0.0 us)

commit v8 on v7

--- a/solution.py
+++ b/solution.py
@@ -40,7 +40,7 @@
 def kernel(
     rows_hbm, vals_hbm, hours_hbm, prior_hbm, trans_hbm, sites_hbm,
     out_ref, sites_out,
-    xs, vs, hs, prior, trans, coupled, power, grams, drives, work, prefix, partner,
+    xs, vs, hs, prior, trans, turned_map, power, drives, work, prefix, partner,
     ydiff, yoff, pre, full, handed, planemap, planeoff, lower, lowermap, entry,
     qhi, qlo, qoff, sin, sout, means,
     load_sem, xsend, xrecv, asend, arecv, csend, crecv, ysend, yrecv, osend, orecv,
@@ -131,11 +131,13 @@
         copy.wait()
 
     transposed = trans[...].T
-    coupled[...] = dot3(split(transposed), split(prior[...]))
+    turned_map[...] = transposed
     power[...] = transposed
     for _ in range(3):
         parts = split(power[...])
         power[...] = dot3(parts, parts)
+
+    square, drive, gain = slice(0, S), slice(S, ROWS), slice(ROWS, ROWS + S)
 
     def add_rows(slot, first):
         hour = hs[slot]
@@ -151,7 +153,7 @@
         for h in range(HR):
             member = jnp.where(hour == h, 1.0, 0.0).astype(BF16)
             product = mm(turned * member, block)
-            grams[h] = product if first else grams[h] + product
+            work[h, gain] = product if first else work[h, gain] + product
 
     add_rows(3, True)
     hear(0)
@@ -180,48 +182,38 @@
     eye = (
         lax.broadcasted_iota(jnp.int32, (S, S), 0) == lax.broadcasted_iota(jnp.int32, (S, S), 1)
     ).astype(F32)
+    scales = []
     for h in range(HR):
-        lam = prior[...] + grams[h]
+        lam = prior[...] + work[h, gain]
         bound = jnp.max(jnp.sum(jnp.abs(lam), axis=0, keepdims=True), axis=1, keepdims=True)
-        scale = 1.0 / bound
-        work[h, 0:S] = eye - lam * scale
-        work[h, S:2 * S] = coupled[...] * scale
-        work[h, 2 * S:2 * S + PAD] = drives[...] * scale
+        scales.append(1.0 / bound)
+        work[h, square] = eye - lam * scales[h]
+        work[h, drive] = drives[...]
 
     def level(k, carry):
         for h in range(HR):
             held = work[h]
-            parts = split(held)
-            factor = (parts[0][0:S], parts[1][0:S])
-            product = dot3(parts, factor)
-            work[h, 0:S] = product[0:S]
-            work[h, S:2 * S + PAD] = held[S:2 * S + PAD] + product[S:2 * S + PAD]
+            high, low = split(held[0:ROWS])
+            rows = jnp.concatenate([high, held[gain].astype(BF16), low], axis=0)
+            first = mm(rows, high[square])
+            exact = first[0:ROWS] + first[ROWS + S:] + mm(high, low[square])
+            work[h, square] = exact[square]
+            work[h, drive] = held[drive] + exact[drive]
+            work[h, gain] = held[gain] + first[gain]
         return carry
 
-    lax.fori_loop(0, NS_ITERS - 2, level, 0)
-
-    def closing(h, last):
-        held = work[h]
-        high, low = split(held)
-        factor = high[0:S]
-        maps = jnp.concatenate([high[S:2 * S + PAD], low[S:2 * S + PAD]], axis=0)
-        both = mm(maps, factor)
-        if not last:
-            square = (factor, low[0:S])
-            work[h, 0:S] = dot3(square, square)
-        work[h, S:2 * S + PAD] = held[S:2 * S + PAD] + both[0:ROWS] + both[ROWS:2 * ROWS]
-
+    lax.fori_loop(0, NS_ITERS, level, 0)
     for h in range(HR):
-        closing(h, False)
-    for h in range(HR):
-        closing(h, True)
+        kept = eye - work[h, square] - work[h, gain] * scales[h]
+        work[h, gain] = dot3(split(turned_map[...]), split(kept))
+        work[h, drive] = work[h, drive] * scales[h]
 
     def after(earlier, later_map, later_off):
         joined = dot3(split(earlier), split(later_map))
         return joined[0:S], joined[S:ROWS] + wide(later_off)
 
     def hour(h):
-        return work[h, S:2 * S], work[h, 2 * S + h:2 * S + h + 1]
+        return work[h, gain], work[h, S + h:S + h + 1]
 
     def put(ref, mapped):
         ref[0:S] = mapped[0]
@@ -446,7 +438,6 @@
             pltpu.VMEM((S, S), F32),
             pltpu.VMEM((S, S), F32),
             pltpu.VMEM((S, S), F32),
-            pltpu.VMEM((HR, S, S), F32),
             pltpu.VMEM((PAD, S), F32),
             pltpu.VMEM((HR, 2 * S + PAD, S), F32),
             pltpu.VMEM((HR, ROWS, S), F32),

time: 59 us -> 58.2 us (0.986)
  Pallas kernels: 58.9 us -> 58.1 us
    pallas_call x1, Pallas kernels: 57.3 us -> 56.5 us  [filtered_means(): pl.pallas_call(kernel, out_shape=(jax.ShapeDtypeStruct((NZ, PLANE, HR, S)...]
where the time goes in v8:
time: 58.2 us; the launch traced here: 58.1 us
  Pallas kernels  58.1 us (100%)
    pallas_call x1, Pallas kernels, filtered_means(): pl.pallas_call(kernel, out_shape=(jax.ShapeDtypeStruct((NZ, PLANE, HR, S)...  56.5 us
    pallas_call x1, Pallas kernels, predict(): pl.pallas_call(predict_kernel, out_shape=jax.ShapeDtypeStruct((hours, sit...  1.64 us

profile of v8, /device:TPU:1, one launch (start us, length us, event | category | flops | bytes accessed | tf_op | source)
XLA Modules:
  0.0 58.1 jit_solution(2841202718850158089)
XLA Ops:
  0.0 56.5 %shard_map.64 = (bf16[8,8,4,256]{3,2,1,0:T(4,128)(2,1)S(1)}, bf16[4096,256]{1,0:T(8,128)(2,1)S(1)}) custom-call(bf16[512,256]{1,0:T(8,128)(2,1)} %rows_hbm.1, bf16[4,128]{1,0:T(4,128)(2,1)} %bitcast.3, s32[1,512]{1,0:T(1,128)} %bitcast.2, f32[256,256]{1,0:T(8,128)} %prior_hbm.1, f32[256,256]{1,0:T(8,128)} %trans_hbm.1, bf16[4096,256]{1,0:T(8,128)(2,1)} %sites_hbm.1), custom_call_target="tpu_custom_call" | custom-call | tf_op jit(solution)/shard_map/pallas_call | solution.py:425
  56.5 1.6 %shard_map.65 = bf16[256,4096]{1,0:T(8,128)(2,1)} custom-call(bf16[256,256]{1,0:T(8,128)(2,1)S(1)} %reshape.7.means_ref, bf16[4096,256]{1,0:T(8,128)(2,1)S(1)} %get-tuple-element.8.sites_ref), custom_call_target="tpu_custom_call" | custom-call | tf_op jit(solution)/shard_map/pallas_call | solution.py:500
  (1 shorter events, 0.0 us)

commit v9 on v8

--- a/solution.py
+++ b/solution.py
@@ -16,6 +16,8 @@
 NX, NY, NC, NZ = 4, 4, 2, 8
 PLANE = NY * NC
 CHUNKS, WIDTH = 8, 512
+SOON = 6
+EARLY = SOON * PLANE * HR
 
 
 def split(a):
@@ -33,13 +35,25 @@
     return mm(ah, bh) + mm(al, bh) + mm(ah, bl)
 
 
+def against(rows, sites):
+    product = lax.dot_general(
+        rows, sites, (((1,), (1,)), ((), ())), preferred_element_type=F32
+    )
+    return product.astype(BF16)
+
+
+def hours_of(means, first, last):
+    blocks = [means[p, b].astype(F32) for p in range(first, last) for b in range(PLANE)]
+    return jnp.concatenate(blocks, axis=0).astype(BF16)
+
+
 def wide(row):
     return jnp.broadcast_to(row, (PAD, S))
 
 
 def kernel(
     rows_hbm, vals_hbm, hours_hbm, prior_hbm, trans_hbm, sites_hbm,
-    out_ref, sites_out,
+    out_ref, sites_out, early_ref,
     xs, vs, hs, prior, trans, turned_map, power, drives, work, prefix, partner,
     ydiff, yoff, pre, full, handed, planemap, planeoff, lower, lowermap, entry,
     qhi, qlo, qoff, sin, sout, means,
@@ -379,14 +393,39 @@
     for j in range(1, PLANE):
         device = (z * PLANE + lax.rem(spot + j, PLANE), x)
         send(mine, mine, psend.at[j - 1], precv.at[j - 1], device)
-    for j in range(1, PLANE):
-        origin = lax.rem(spot + PLANE - j, PLANE)
-        arrived(means.at[z, origin], psend.at[j - 1], precv.at[j - 1])
-    for k in (1, 7, 2, 6, 3, 5, 4):
-        origin = lax.rem(z + NZ - k, NZ)
-        arrived(means.at[origin], zsend.at[k - 1], zrecv.at[k - 1])
+    held_sites.wait()
+
+    def plane_here():
+        for j in range(1, PLANE):
+            origin = lax.rem(spot + PLANE - j, PLANE)
+            arrived(means.at[z, origin], psend.at[j - 1], precv.at[j - 1])
+
+    def plane_from(origin):
+        @pl.when(z != origin)
+        def _():
+            slot = lax.rem(z + NZ - origin + NZ - 1, NZ)
+            slot = jnp.minimum(slot, NZ - 2)
+            arrived(means.at[origin], zsend.at[slot], zrecv.at[slot])
+
+    @pl.when(z < SOON)
+    def _():
+        plane_here()
+
+    for origin in range(SOON):
+        plane_from(origin)
+    rows = hours_of(means, 0, SOON)
+    for c in range(CHUNKS):
+        early_ref[:, c * WIDTH:(c + 1) * WIDTH] = against(
+            rows, sites_out[c * WIDTH:(c + 1) * WIDTH, :]
+        )
+
+    @pl.when(z >= SOON)
+    def _():
+        plane_here()
+
+    for origin in range(SOON, NZ):
+        plane_from(origin)
     out_ref[...] = means[...]
-    held_sites.wait()
 
     for copy in started:
         copy.wait_send()
@@ -427,9 +466,10 @@
         out_shape=(
             jax.ShapeDtypeStruct((NZ, PLANE, HR, S), BF16),
             jax.ShapeDtypeStruct(site_basis.shape, BF16),
+            jax.ShapeDtypeStruct((EARLY, site_basis.shape[0]), BF16),
         ),
         in_specs=[any_space] * 6,
-        out_specs=(pl.BlockSpec(memory_space=pltpu.VMEM),) * 2,
+        out_specs=(pl.BlockSpec(memory_space=pltpu.VMEM),) * 3,
         scratch_shapes=[
             pltpu.VMEM((4, 2, 256, S), BF16),
             pltpu.VMEM((4, 4, 128), BF16),
@@ -479,42 +519,45 @@
     ))
 
 
-def predict_kernel(means_ref, sites_ref, out_hbm, held, sems):
-    copies = []
+def predict_kernel(means_ref, sites_ref, early_ref, out_hbm, held, sems):
+    copies = [pltpu.make_async_copy(early_ref, out_hbm.at[pl.ds(0, EARLY)], sems.at[CHUNKS])]
+    copies[0].start()
+    late = hours_of(means_ref, SOON, NZ)
     for c in range(CHUNKS):
-        held[c] = lax.dot_general(
-            means_ref[...], sites_ref[c * WIDTH:(c + 1) * WIDTH, :],
-            (((1,), (1,)), ((), ())), preferred_element_type=F32,
-        ).astype(BF16)
+        held[c] = against(late, sites_ref[c * WIDTH:(c + 1) * WIDTH, :])
         copies.append(
-            pltpu.make_async_copy(held.at[c], out_hbm.at[:, pl.ds(c * WIDTH, WIDTH)], sems.at[c])
+            pltpu.make_async_copy(
+                held.at[c],
+                out_hbm.at[pl.ds(EARLY, late.shape[0]), pl.ds(c * WIDTH, WIDTH)],
+                sems.at[c],
+            )
         )
         copies[-1].start()
     for copy in copies:
         copy.wait()
 
 
-def predict(means, site_basis):
+def predict(means, sites, early):
     vmem = pl.BlockSpec(memory_space=pltpu.MemorySpace.VMEM)
-    hours, sites = means.shape[0], site_basis.shape[0]
+    hours = NZ * PLANE * HR
     return pl.pallas_call(
         predict_kernel,
-        out_shape=jax.ShapeDtypeStruct((hours, sites), BF16),
-        in_specs=[vmem, vmem],
+        out_shape=jax.ShapeDtypeStruct((hours, sites.shape[0]), BF16),
+        in_specs=[vmem] * 3,
         out_specs=pl.BlockSpec(memory_space=pltpu.MemorySpace.HBM),
         scratch_shapes=[
-            pltpu.VMEM((CHUNKS, hours, WIDTH), BF16),
-            pltpu.SemaphoreType.DMA((CHUNKS,)),
+            pltpu.VMEM((CHUNKS, hours - EARLY, WIDTH), BF16),
+            pltpu.SemaphoreType.DMA((CHUNKS + 1,)),
         ],
         compiler_params=pltpu.CompilerParams(vmem_limit_bytes=16 * 1024 * 1024),
-    )(means, site_basis)
+    )(means, sites, early)
 
 
 def body(obs_rows, obs_values, obs_hours, prior_precision, transition, site_basis):
-    means, sites = filtered_means(
+    means, sites, early = filtered_means(
         obs_rows, obs_values, obs_hours, prior_precision, transition, site_basis
     )
-    return predict(means.reshape(NZ * PLANE * HR, S), sites)
+    return predict(means, sites, early)
 
 
 def solution(mesh):

time: 58.2 us -> 58 us (level)
  no operation moved by 1% of the time
where the time goes in v9:
time: 58 us; the launch traced here: 57.9 us
  Pallas kernels  57.9 us (100%)
    pallas_call x1, Pallas kernels, filtered_means(): pl.pallas_call(kernel, out_shape=(jax.ShapeDtypeStruct((NZ, PLANE, HR, S)...  56.4 us
    pallas_call x1, Pallas kernels, predict(): pl.pallas_call(predict_kernel, out_shape=jax.ShapeDtypeStruct((hours, sit...  1.47 us

profile of v9, /device:TPU:1, one launch (start us, length us, event | category | flops | bytes accessed | tf_op | source)
XLA Modules:
  0.0 57.9 jit_solution(14188701863262767624)
XLA Ops:
  0.0 56.4 %shard_map.64 = (bf16[8,8,4,256]{3,2,1,0:T(4,128)(2,1)S(1)}, bf16[4096,256]{1,0:T(8,128)(2,1)S(1)}, bf16[192,4096]{1,0:T(8,128)(2,1)S(1)}) custom-call(bf16[512,256]{1,0:T(8,128)(2,1)} %rows_hbm.1, bf16[4,128]{1,0:T(4,128)(2,1)} %bitcast.3, s32[1,512]{1,0:T(1,128)} %bitcast.2, f32[256,256]{1,0:T(8,128)} %prior_hbm.1, f32[256,256]{1,0:T(8,128)} %trans_hbm.1, ...), custom_call_target="tpu_custom_call" | custom-call | tf_op jit(solution)/shard_map/pallas_call | solution.py:464
  56.4 1.5 %shard_map.65 = bf16[256,4096]{1,0:T(8,128)(2,1)} custom-call(bf16[8,8,4,256]{3,2,1,0:T(4,128)(2,1)S(1)} %get-tuple-element.8.means_ref, bf16[4096,256]{1,0:T(8,128)(2,1)S(1)} %get-tuple-element.9.sites_ref, bf16[192,4096]{1,0:T(8,128)(2,1)S(1)} %get-tuple-element.10.early_ref), custom_call_target="tpu_custom_call" | custom-call | tf_op jit(solution)/shard_map/pallas_call | solution.py:543

commit v10 on v9

--- a/solution.py
+++ b/solution.py
@@ -423,9 +423,6 @@
     def _():
         plane_here()
 
-    for origin in range(SOON, NZ):
-        plane_from(origin)
-    out_ref[...] = means[...]
 
     for copy in started:
         copy.wait_send()
@@ -456,6 +453,10 @@
     def _():
         for copy in to_odd:
             copy.wait_send()
+
+    for origin in range(SOON, NZ):
+        plane_from(origin)
+    out_ref[...] = means[...]
 
 
 def filtered_means(obs_rows, obs_values, obs_hours, prior_precision, transition, site_basis):

time: 58 us -> 57.9 us (level)
  no operation moved by 1% of the time
where the time goes in v10:
time: 57.9 us
  Pallas kernels  57.9 us (100%)
    pallas_call x1, Pallas kernels, filtered_means(): pl.pallas_call(kernel, out_shape=(jax.ShapeDtypeStruct((NZ, PLANE, HR, S)...  56.4 us
    pallas_call x1, Pallas kernels, predict(): pl.pallas_call(predict_kernel, out_shape=jax.ShapeDtypeStruct((hours, sit...  1.46 us

profile of v10, /device:TPU:1, one launch (start us, length us, event | category | flops | bytes accessed | tf_op | source)
XLA Modules:
  0.0 57.9 jit_solution(2489489094243372321)
XLA Ops:
  0.0 56.4 %shard_map.64 = (bf16[8,8,4,256]{3,2,1,0:T(4,128)(2,1)S(1)}, bf16[4096,256]{1,0:T(8,128)(2,1)S(1)}, bf16[192,4096]{1,0:T(8,128)(2,1)S(1)}) custom-call(bf16[512,256]{1,0:T(8,128)(2,1)} %rows_hbm.1, bf16[4,128]{1,0:T(4,128)(2,1)} %bitcast.3, s32[1,512]{1,0:T(1,128)} %bitcast.2, f32[256,256]{1,0:T(8,128)} %prior_hbm.1, f32[256,256]{1,0:T(8,128)} %trans_hbm.1, ...), custom_call_target="tpu_custom_call" | custom-call | tf_op jit(solution)/shard_map/pallas_call | solution.py:465
  56.4 1.5 %shard_map.65 = bf16[256,4096]{1,0:T(8,128)(2,1)} custom-call(bf16[8,8,4,256]{3,2,1,0:T(4,128)(2,1)S(1)} %get-tuple-element.8.means_ref, bf16[4096,256]{1,0:T(8,128)(2,1)S(1)} %get-tuple-element.9.sites_ref, bf16[192,4096]{1,0:T(8,128)(2,1)S(1)} %get-tuple-element.10.early_ref), custom_call_target="tpu_custom_call" | custom-call | tf_op jit(solution)/shard_map/pallas_call | solution.py:544
